TPU v7x, 32 devices: a whole 2x2x4 slice. The times are simulated.
32 devices in a mesh: group: 2 (over y), inst: 4 (over x, core), brick: 4 (over z).
Axes of the slice: x: 2, y: 2, z: 4, core: 2. Of those that a mesh axis runs over, the one named last changes fastest.
Arguments:
- state: float32 [32, 5, 32, 4096], P(('group', 'inst'), None, 'brick'), parts along dimension 0, may hold values from -1.5 to 4, as said below
- time_step: float32 [64, 4096], P(('group', 'brick')), parts along dimension 0, may hold values from 0.05 to 0.5
- blocks: bfloat16 [8, 320, 320], replicated, may hold values from -0.3125 to 0.3125
- cut_counts: int32 [8], P('group'), parts along dimension 0, may hold values from 1 to 256, 384 in all
- tile_index: int32 [8, 256], P(('group', 'brick')), parts along dimension 0, may hold values from 0 to 511, as said below
- tile_type: int32 [8, 256], P(('group', 'brick')), parts along dimension 0, may hold values from 0 to 7
Outputs:
- residual: float32 [32, 5, 32, 4096], P(('group', 'inst'), None, 'brick'), parts along dimension 0
- new_state: float32 [32, 5, 32, 4096], P(('group', 'inst'), None, 'brick'), parts along dimension 0
There are 2 independent parts, one for each index of `group`. A program takes and returns all parts, laid end to end along the dimension named above; an argument that names none is the same for every part. Nothing has to cross between parts.
Inputs may be any that keep to these rules, and one draw needn't show every extreme that they name: `state`: component 0 (density) lies in 0.5 to 2, components 1 to 3 in -1.5 to 1.5, component 4 in 1.5 to 4. `tile_index`: row b lists 256 different tiles of brick b. `cut_counts`: the entries sum to 384.
All inputs are finite; a program needn't handle non-finite values.
Results may differ from a plain program's by a relative error of at most 0.0013.
Values may be sent and summed in bfloat16 or wider, within the bound.
No kernel may reach another device: no remote copies, remote signals or barrier semaphores. Data moves between devices by JAX's collectives and lax.ppermute only.
A program may use at most 64 MiB of HBM per device.

v0:
```python
import jax
import jax.numpy as jnp
from jax import lax
from jax.sharding import PartitionSpec as P

NINST = 16
NVAR = 5
TILE = 64
TSIZE = 320
TILES_DEV = 512


GAMMA_MINUS = 0.4
EPS_FOURTH = 0.03125


def padded(cells, sides, width):
    for axis, dim in sides:
        count = lax.axis_size(axis)
        ends = count - 1
        head = lax.slice_in_dim(cells, 0, width, axis=dim)
        tail = lax.slice_in_dim(cells, cells.shape[dim] - width, cells.shape[dim], axis=dim)
        cells = jnp.concatenate(
            [
                lax.ppermute(tail, axis, [(i, (i + 1) % count) for i in range(ends)]),
                cells,
                lax.ppermute(head, axis, [((i + 1) % count, i) for i in range(ends)]),
            ],
            axis=dim,
        )
    return cells


def spectral_entry(diff, count):
    shifted = jnp.mod(diff, count)
    sign = 1.0 - 2.0 * jnp.mod(diff, 2).astype(jnp.float32)
    safe = jnp.where(shifted == 0, 1, shifted).astype(jnp.float32)
    value = sign / jnp.tan(jnp.pi * safe / count)
    return jnp.where(shifted == 0, 0.0, value)


def euler_flux(state):
    density = state[:, 0]
    density = jnp.where(density == 0.0, 1.0, density)
    mom_one = state[:, 1]
    mom_two = state[:, 2]
    mom_three = state[:, 3]
    energy = state[:, 4]
    speed = mom_one / density
    press = GAMMA_MINUS * (
        energy - 0.5 * (mom_one * mom_one + mom_two * mom_two + mom_three * mom_three) / density
    )
    return jnp.stack(
        [
            mom_one,
            mom_one * speed + press,
            mom_two * speed,
            mom_three * speed,
            (energy + press) * speed,
        ],
        axis=1,
    )


def apply_range(states, kinds_row, blocks, lower, upper):
    rows = states.shape[0]
    row_ids = jnp.arange(rows, dtype=jnp.int32)
    keep = (row_ids >= lower) & (row_ids < upper)
    total = jnp.zeros(states.shape, jnp.float32)
    for kind in range(blocks.shape[0]):
        select = keep & (kinds_row == kind)
        masked = jnp.where(select[:, None, None], states, jnp.zeros_like(states))
        total = total + jnp.einsum(
            "ab,tib->tia", blocks[kind], masked, preferred_element_type=jnp.float32
        )
    return total


def per_device(state, time_step, blocks, cut_counts, tile_index, tile_type):
    inst_here = state.shape[0]
    rows_here = state.shape[2]
    row_cells = state.shape[3]
    qpad = padded(state.astype(jnp.bfloat16), (("brick", 2),), 2).astype(state.dtype)
    fpad = euler_flux(qpad)
    transport = 0.5 * (fpad[:, :, 3:-1] - fpad[:, :, 1:-3])
    smoothing = EPS_FOURTH * (
        qpad[:, :, 4:]
        - 4.0 * qpad[:, :, 3:-1]
        + 6.0 * qpad[:, :, 2:-2]
        - 4.0 * qpad[:, :, 1:-3]
        + qpad[:, :, :-4]
    )
    mine = lax.axis_index("inst") * inst_here + jnp.arange(inst_here, dtype=jnp.int32)
    piece = lax.all_gather(state, "inst", axis=0, tiled=True)
    others = jnp.arange(piece.shape[0], dtype=jnp.int32)
    coef = spectral_entry(mine[:, None] - others[None, :], NINST)
    timewise = jnp.einsum("jk,kcxs->jcxs", coef, piece, precision=lax.Precision.HIGHEST)
    tiles = (
        state.reshape(inst_here, NVAR, TILES_DEV, TILE)
        .transpose(2, 0, 1, 3)
        .reshape(TILES_DEV, inst_here, TSIZE)
    )
    index_row = tile_index[0]
    kinds_row = tile_type[0]
    own_states = tiles[index_row].astype(jnp.bfloat16)
    brick_here = lax.axis_index("brick")
    count_here = cut_counts[brick_here]
    results = apply_range(own_states, kinds_row, blocks, 0, count_here)
    cut_tiles = jnp.zeros((TILES_DEV, inst_here, TSIZE), jnp.float32).at[index_row].add(results)
    cut = (
        cut_tiles.reshape(TILES_DEV, inst_here, NVAR, TILE)
        .transpose(1, 2, 0, 3)
        .reshape(inst_here, NVAR, rows_here, row_cells)
    )
    residual = transport + smoothing + cut + timewise
    new_state = state - time_step[None, None] * residual
    return (residual, new_state)


def solution(mesh):
    placed = (
        P(("group", "inst"), None, "brick", None),
        P(("group", "brick"), None),
        P(),
        P("group"),
        P(("group", "brick"), None),
        P(("group", "brick"), None),
    )
    return jax.shard_map(
        per_device,
        mesh=mesh,
        in_specs=placed,
        out_specs=(
            P(("group", "inst"), None, "brick", None),
            P(("group", "inst"), None, "brick", None),
        ),
        check_vma=False,
    )
```

profile of v0, /device:TPU:0, one launch (start us, length us, event | category | flops | bytes accessed | tf_op | source)
XLA Modules:
  0.0 146.6 jit_solution(6179582172153618926)
XLA Ops:
  7.2 0.0 copy-start.1
  7.2 0.0 all-gather.2.cloned.1.call-start
  7.2 0.7 all-gather.2.cloned.1.call-update
  7.9 1.0 copy-done.1
  8.9 1.7 %copy.75 = bf16[4,5,8,4096]{3,0,2,1:T(4,128)(2,1)S(1)} copy(f32[4,5,8,4096]{3,2,1,0:T(8,128)S(1)} %copy-done.1) | data formatting | bytes 3932160 | tf_op args[0]
  10.6 0.0 copy-start.2
  10.6 1.0 copy-done.2
  11.7 1.1 fusion.82
  12.8 5.7 %collective-permute-start = (bf16[4,5,2,4096]{3,0,2,1:T(4,128)(2,1)}, bf16[4,5,2,4096]{3,0,2,1:T(4,128)(2,1)}, u32[]{:S(2)}, u32[]{:S(2)}) collective-permute-start(bf16[4,5,2,4096]{3,0,2,1:T(4,128)(2,1)} %get-tuple-element.19), channel_id=1, source_target_pairs={{0,1},{1,2},{2,3},{4,5},{5,6},{6,7},{8,9},{9,10},{10,11},{12,13},{... | collective-permute-start | bytes 983048 | tf_op jit(solution)/shard_map/ppermute | solution.py:25
  18.5 1.5 collective-permute-start.1
  19.9 3.5 %reshape.131 = bf16[4,5,512,64]{3,2,1,0:T(8,128)(2,1)} reshape(f32[4,5,8,4096]{3,2,1,0:T(8,128)S(1)} %copy-done.1) | data formatting | bytes 3932160 | tf_op jit(solution)/shard_map/reshape | solution.py:99
  23.4 0.0 copy-start.7
  23.4 0.0 copy-start.5
  23.4 4.3 %copy.33 = bf16[512,4,5,64]{0,3,2,1:T(8,128)(2,1)} copy(bf16[512,4,5,64]{3,0,2,1:T(8,128)(2,1)} %bitcast.52) | data formatting | bytes 2621440 | tf_op jit(solution)/shard_map/transpose | solution.py:100
  27.7 0.0 copy-start.4
  27.7 3.5 %copy.34 = bf16[512,4,320]{2,1,0:T(4,128)(2,1)} copy(bf16[512,4,320]{0,2,1:T(8,128)(2,1)} %bitcast.54) | data formatting | bytes 2621440 | tf_op jit(solution)/shard_map/reshape | solution.py:101
  31.3 0.0 copy-done.7
  31.3 0.6 dynamic_slice.3
  31.9 0.0 copy-done.5
  31.9 2.9 %gather_fusion = bf16[256,4,320]{2,1,0:T(4,128)(2,1)S(1)} fusion(bf16[512,4,320]{2,1,0:T(4,128)(2,1)} %copy.34, s32[1024]{0:T(1024)S(1)} %pad_clamp_fusion), kind=kCustom, calls=%fused_computation | custom fusion | bytes 1311744 | tf_op jit(solution)/shard_map/gather | solution.py:105
  34.8 0.0 copy-done.4
  34.9 0.7 fusion.64
  35.5 0.7 fusion.66
  36.2 0.7 fusion.68
  36.9 0.7 fusion.70
  37.5 0.0 copy-start.3
  37.5 4.3 %broadcast_select_fusion = (bf16[256,4,320]{2,1,0:T(4,128)(2,1)S(1)}, bf16[256,4,320]{2,1,0:T(4,128)(2,1)S(1)}, bf16[256,4,320]{2,1,0:T(4,128)(2,1)S(1)}, bf16[2...) fusion(bf16[256,4,320]{2,1,0:T(4,128)(2,1)S(1)} %gather_fusion,, ...), kind=kLoop, calls=%fused_computation.42 | loop fusion | flops 2621440 | bytes 5900288 | tf_op jit(solution)/shard_map/jit(_where)/select_n | solution.py:72
  41.9 0.0 copy-done.3
  41.9 0.5 fusion.19
  42.4 0.5 convolution_add_fusion.6
  43.0 0.5 convolution_add_fusion.5
  43.5 0.5 convolution_add_fusion.4
  44.1 0.5 convolution_add_fusion.3
  44.6 0.5 convolution_add_fusion.2
  45.2 0.5 convolution_add_fusion.1
  45.7 1.6 %convolution_add_fusion = f32[256,4,320]{0,2,1:T(8,128)} fusion(f32[256,4,320]{0,2,1:T(8,128)S(1)} %convolution_add_fusion.1, bf16[256,4,320]{2,1,0:T(4,128)(2,1)S(1)} %get-tuple-element.21, bf16[8,320,320]{2,1,0:T(8,128)(2,1)S(1)} %copy-done.3), kind=kOutput, calls=%fused_computation.21 | convolution fusion | flops 210042880 | bytes 3653632 | tf_op jit(solution)/shard_map/ab,tib->tia/dot_general | solution.py:73
  47.3 2.5 %copy.43 = f32[256,4,320]{2,1,0:T(4,128)} copy(f32[256,4,320]{0,2,1:T(8,128)} %convolution_add_fusion) | data formatting | bytes 2621440 | tf_op jit(solution)/shard_map/add | solution.py:73
  49.8 2.2 %broadcast_in_dim.70 = f32[512,4,320]{2,1,0:T(4,128)} broadcast(f32[]{:T(128)} %constant.23.clone.1), dimensions={} | broadcast | bytes 2621444 | tf_op jit(solution)/shard_map/broadcast_in_dim | solution.py:109
  52.0 32.5 %scatter_fusion = f32[512,4,320]{2,1,0:T(4,128)} fusion(f32[512,4,320]{2,1,0:T(4,128)} %broadcast_in_dim.70, s32[256]{0:T(256)S(1)} %bitcast.56, f32[256,4,320]{2,1,0:T(4,128)} %copy.43), kind=kCustom, calls=%fused_computation.1 | custom fusion | flops 327680 | bytes 3933184 | tf_op jit(solution)/shard_map/scatter-add | solution.py:109
  84.5 4.7 %copy.44 = f32[512,4,320]{0,2,1:T(8,128)} copy(f32[512,4,320]{2,1,0:T(4,128)} %scatter_fusion) | data formatting | bytes 5242880 | tf_op jit(solution)/shard_map/scatter-add | solution.py:109
  89.2 4.9 %copy.45 = f32[4,5,512,64]{3,2,1,0:T(8,128)} copy(f32[4,5,512,64]{2,3,1,0:T(8,128)} %bitcast.53) | data formatting | bytes 5242880 | tf_op jit(solution)/shard_map/transpose | solution.py:112
  94.1 5.4 %reshape.134 = f32[4,5,8,4096]{3,2,1,0:T(8,128)} reshape(f32[4,5,512,64]{3,2,1,0:T(8,128)} %copy.45) | data formatting | bytes 5242880 | tf_op jit(solution)/shard_map/reshape | solution.py:113
  99.4 0.0 collective-permute-done
  99.4 0.0 collective-permute-done.1
  99.5 2.5 %maximum_convert_fusion = f32[4,5,12,4096]{3,0,2,1:T(4,128)S(1)} fusion(bf16[4,5,2,4096]{3,0,2,1:T(4,128)(2,1)} %collective-permute-done.1, bf16[4,5,8,4096]{3,0,2,1:T(4,128)(2,1)} %copy-done.2, bf16[4,5,2,4096]{3,0,2,1:T(4,128)(2,1)} %collective-permute-done), kind=kLoop, calls=%fused_computation.20 | loop fusion | flops 2949120 | bytes 5898240 | tf_op jit(solution)/shard_map/convert_element_type | solution.py:83
  102.0 0.0 copy-start
  102.0 1.0 slice_dynamic-update-slice_fusion
  103.0 1.9 %add_dynamic-update-slice_fusion = (f32[4,5,12,4096]{3,0,2,1:T(4,128)}, f32[4,1,12,4096]{3,0,2,1:T(4,128)S(1)}, f32[4,1,12,4096]{3,0,2,1:T(4,128)S(1)}) fusion(f32[4,5,12,4096]{3,0,2,1:T(4,128)} %slice_dynamic-update-slice_fusion, f32[4,5,12,4096]{3,0,2,1:T(4,128)S(1)} %maximum_convert_fusion), kind=kLoop, calls=%fused_computation.40 | loop fusion | flops 2752512 | bytes 6291456
  104.9 1.1 multiply_dynamic-update-slice_fusion.2
  106.0 0.0 copy-start.6
  106.0 1.1 multiply_dynamic-update-slice_fusion.1
  107.1 0.0 copy-done
  107.1 1.2 multiply_dynamic-update-slice_fusion
  108.3 0.0 all-gather.2.cloned.1.call-done
  108.3 0.0 copy-done.6
  108.3 25.4 %multiply_subtract_fusion = (f32[4,5,8,4096]{3,0,2,1:T(4,128)S(1)}, f32[4,5,8,4096]{3,0,2,1:T(4,128)S(1)}) fusion(f32[4,5,8,4096]{3,2,1,0:T(8,128)S(1)} %copy-done.1, f32[8,4096]{1,0:T(8,128)S(1)} %copy-done.6, f32[16,5,8,4096]{3,2,1,0:T(8,128)} %all-gather.2.cloned.1.call-done, s32[4]{0:T(128)S(1)} %iota_add_fusion, f32[4,5,8,4096]{3,2,1,0:T(8,128)} %reshape.134, ...), kind=kOutput, calls=%fused_computation.17 | convolution fusion | flops 135661376 | bytes 39452688 | tf_op jit(solution)/shard_map/jk,kcxs->jcxs/dot_general | solution.py:97
  133.7 3.0 %copy.49 = f32[4,5,8,4096]{3,2,1,0:T(8,128)} copy(f32[4,5,8,4096]{3,0,2,1:T(4,128)S(1)} %get-tuple-element.30) | data formatting | bytes 5242880
  136.7 3.0 %copy.50 = f32[4,5,8,4096]{3,2,1,0:T(8,128)} copy(f32[4,5,8,4096]{3,0,2,1:T(4,128)S(1)} %get-tuple-element.29) | data formatting | bytes 5242880
  (4 shorter events, 0.1 us)
Async XLA Ops:
  7.2 1.7 %copy-start.1 = (f32[4,5,8,4096]{3,2,1,0:T(8,128)S(1)}, f32[4,5,8,4096]{3,2,1,0:T(8,128)}, u32[]{:S(2)}) copy-start(f32[4,5,8,4096]{3,2,1,0:T(8,128)} %param.6) | copy-start | bytes 7864324
  7.2 101.1 %all-gather.2.cloned.1.call-start = ((), (), s32[]{:S(2)}) async-start(), calls=%async_computation | async-start | bytes 13107200 | tf_op jit(solution)/shard_map/all_gather | solution.py:94
  10.6 1.1 copy-start.2
  12.8 86.7 %collective-permute-start = (bf16[4,5,2,4096]{3,0,2,1:T(4,128)(2,1)}, bf16[4,5,2,4096]{3,0,2,1:T(4,128)(2,1)}, u32[]{:S(2)}, u32[]{:S(2)}) collective-permute-start(bf16[4,5,2,4096]{3,0,2,1:T(4,128)(2,1)} %get-tuple-element.19), channel_id=1, source_target_pairs={{0,1},{1,2},{2,3},{4,5},{5,6},{6,7},{8,9},{9,10},{10,11},{12,13},{... | collective-permute-start | bytes 983048 | tf_op jit(solution)/shard_map/ppermute | solution.py:25
  18.5 81.0 %collective-permute-start.1 = (bf16[4,5,2,4096]{3,0,2,1:T(4,128)(2,1)}, bf16[4,5,2,4096]{3,0,2,1:T(4,128)(2,1)}, u32[]{:S(2)}, u32[]{:S(2)}) collective-permute-start(bf16[4,5,2,4096]{3,0,2,1:T(4,128)(2,1)} %get-tuple-element.20), channel_id=1, source_target_pairs={{1,0},{2,1},{3,2},{5,4},{6,5},{7,6},{9,8},{10,9},{11,10},{13,12},{... | collective-permute-start | bytes 983048 | tf_op jit(solution)/shard_map/ppermute | solution.py:27
  23.4 7.8 %copy-start.7 = (s32[4]{0:T(128)S(1)}, s32[4]{0:T(128)}, u32[]{:S(2)}) copy-start(s32[4]{0:T(128)} %param.9) | copy-start | bytes 52
  23.4 8.4 %copy-start.5 = (s32[1,256]{1,0:T(1,128)S(1)}, s32[1,256]{1,0:T(1,128)}, u32[]{:S(2)}) copy-start(s32[1,256]{1,0:T(1,128)} %param.10) | copy-start | bytes 3076
  27.7 7.1 %copy-start.4 = (s32[1,256]{1,0:T(1,128)S(1)}, s32[1,256]{1,0:T(1,128)}, u32[]{:S(2)}) copy-start(s32[1,256]{1,0:T(1,128)} %param.11) | copy-start | bytes 3076
  37.5 4.4 %copy-start.3 = (bf16[8,320,320]{2,1,0:T(8,128)(2,1)S(1)}, bf16[8,320,320]{2,1,0:T(8,128)(2,1)}, u32[]{:S(2)}) copy-start(bf16[8,320,320]{2,1,0:T(8,128)(2,1)} %param.8) | copy-start | bytes 4915204
  102.0 5.1 %copy-start = (f32[4,5,12,4096]{3,0,2,1:T(4,128)}, f32[4,5,12,4096]{3,0,2,1:T(4,128)S(1)}, u32[]{:S(2)}) copy-start(f32[4,5,12,4096]{3,0,2,1:T(4,128)S(1)} %maximum_convert_fusion) | copy-start | bytes 11796484
  106.0 2.3 %copy-start.6 = (f32[8,4096]{1,0:T(8,128)S(1)}, f32[8,4096]{1,0:T(8,128)}, u32[]{:S(2)}) copy-start(f32[8,4096]{1,0:T(8,128)} %param.7) | copy-start | bytes 393220
Sparse Core Ops, SparseCore 0:
  9.5 72.8 all-gather.1
where the time goes:
time: 148 us; the launch traced here: 147 us
  other arithmetic  47.3 us (32%)
  local copies, waits for them, and re-layouts  46.4 us (31%)
  matrix products  30.8 us (21%)
  between operations  14.2 us (10%)
  starting transfers between devices  7.17 us (5%)
    scatter-add x1, other arithmetic, per_device(): jnp.zeros((TILES_DEV, inst_here, TSIZE), jnp.float32).at[index_row]  32.5 us
    dot_general x1, matrix products, per_device(): jnp.einsum('jk,kcxs->jcxs', coef, piece, precision=lax.Precision.HIGHEST)  25.4 us
    unnamed x20, local copies, waits for them, and re-layouts  10.8 us
    ppermute x1, starting transfers between devices, padded(): lax.ppermute(tail, axis, [(i, (i + 1) % count) for i in range(ends)])  5.68 us
    reshape x1, local copies, waits for them, and re-layouts, per_device(): cut = cut_tiles.reshape(TILES_DEV, inst_here, NVAR, TILE).transpose(1, 2,...  5.37 us
    dot_general x8, matrix products, apply_range(): jnp.einsum('ab,tib->tia', blocks[kind], masked, preferred_element_type=jn...  5.37 us
    transpose x1, local copies, waits for them, and re-layouts, per_device(): cut = cut_tiles.reshape(TILES_DEV, inst_here, NVAR, TILE).transpose(1, 2,...  4.86 us
    scatter-add x1, local copies, waits for them, and re-layouts, per_device(): jnp.zeros((TILES_DEV, inst_here, TSIZE), jnp.float32).at[index_row]  4.68 us
  transfers between devices with their start and end apart: 3, of which 0 were waited for; matrix products, arithmetic and copies ran while one was open for 62% of the time, Pallas kernels for 0%

commit v1 on v0

v1 whole, which is shorter than its diff:
```python
import functools
import math

import jax
import jax.numpy as jnp
from jax import lax
from jax.experimental import pallas as pl
from jax.experimental.pallas import tpu as pltpu
from jax.sharding import PartitionSpec as P

TILE = 64
GAMMA_MINUS = 0.4
EPS_FOURTH = 0.03125
LANES = 128
MIB = 1 << 20
CENTRE = (1.25, 0.0, 0.0, 0.0, 2.75)
STATE_VARS = (1, 2)
SUM_GROUPS = ((3, 4), (0,))

IN_VMEM = pl.BlockSpec(memory_space=pltpu.VMEM)
IN_HBM = pl.BlockSpec(memory_space=pltpu.HBM)
IN_SMEM = pl.BlockSpec(memory_space=pltpu.SMEM)


def params(mib):
    return pltpu.CompilerParams(vmem_limit_bytes=mib * MIB)


def spectral(m, period):
    m = m % period
    if m == 0:
        return 0.0
    return (-1.0) ** m / math.tan(math.pi * m / period)


def row_coefs(j, inst, period, base, parity):
    own = [spectral(base * inst + j - k, period) for k in range(inst)]
    even = [spectral((base - 1) * inst + j - k, period) for k in range(inst)]
    odd = [spectral((base + 1) * inst + j - k, period) for k in range(inst)]
    mate = [jnp.where(parity == 0, jnp.float32(a), jnp.float32(b)) for a, b in zip(even, odd)]
    return own + mate


def weighted(coefs, values):
    total = None
    for c, x in zip(coefs, values):
        if isinstance(c, float) and c == 0.0:
            continue
        total = c * x if total is None else total + c * x
    return total


def centred(x, v):
    return x - CENTRE[v] if CENTRE[v] else x


def columns(cells, width, body):
    def one(c, carry):
        body(pl.ds(pl.multiple_of(c * width, width), width), c)
        return carry

    lax.fori_loop(0, cells // width, one, 0)


def pack_state_kernel(state_ref, out_ref, held_ref, sems):
    inst, _, _, cells = state_ref.shape
    chunks = sems.shape[0]
    width = cells // chunks
    lo, hi = STATE_VARS[0], STATE_VARS[-1] + 1
    copies = []
    for c in range(chunks):
        cols = pl.ds(c * width, width)
        copies.append(pltpu.make_async_copy(state_ref.at[:, lo:hi, :, cols], held_ref.at[:, :, :, cols], sems.at[c]))
        copies[-1].start()
    for c in range(chunks):
        copies[c].wait()

        def body(cols, _, base=c * width):
            at = pl.ds(pl.multiple_of(base + cols.start, LANES), LANES)
            for n, v in enumerate(STATE_VARS):
                packed = jnp.concatenate([centred(held_ref[k, n, :, at], v) for k in range(inst)], axis=0)
                out_ref[n, :, at] = packed.astype(jnp.bfloat16)

        columns(width, LANES, body)


def pack_state(state, chunks=2):
    inst, _, rows, cells = state.shape
    n = len(STATE_VARS)
    return pl.pallas_call(
        pack_state_kernel,
        in_specs=[IN_HBM],
        out_specs=IN_VMEM,
        out_shape=pltpu.VMEM((n, inst * rows, cells), jnp.bfloat16),
        scratch_shapes=[pltpu.VMEM((inst, n, rows, cells), jnp.float32), pltpu.SemaphoreType.DMA((chunks,))],
        compiler_params=params(4),
        name="pack_state",
    )(state)


def pack_edges_kernel(state_ref, held_ref, first_ref, second_ref, sems):
    inst, nvar, rows, cells = state_ref.shape
    chunks = sems.shape[0]
    width = cells // chunks
    odd = lax.axis_index("brick") % 2 == 1
    copies = []
    for c in range(chunks):
        cols = pl.ds(c * width, width)
        copies.append(pltpu.make_async_copy(state_ref.at[:, :, :, cols], held_ref.at[:, :, :, cols], sems.at[c]))
        copies[-1].start()
    pair = lax.broadcasted_iota(jnp.int32, (rows, LANES), 0) // 2
    for c in range(chunks):
        copies[c].wait()

        def body(cols, _, base=c * width):
            at = pl.ds(pl.multiple_of(base + cols.start, LANES), LANES)
            for v in range(nvar):
                q = [held_ref[j, v, :, at] for j in range(inst)]
                head, tail = q[0], pltpu.roll(q[0], 2, 0)
                for j in range(1, inst):
                    head = jnp.where(pair == j, pltpu.roll(q[j], 2 * j, 0), head)
                    tail = jnp.where(pair == j, pltpu.roll(q[j], (2 * j + 2) % rows, 0) if (2 * j + 2) % rows else q[j], tail)
                first_ref[v, :, at] = jnp.where(odd, head, tail).astype(jnp.bfloat16)
                second_ref[v, :, at] = jnp.where(odd, tail, head).astype(jnp.bfloat16)

        columns(width, LANES, body)


def pack_edges(state, chunks=2):
    _, nvar, rows, cells = state.shape
    edge = pltpu.VMEM((nvar, rows, cells), jnp.bfloat16)
    return pl.pallas_call(
        pack_edges_kernel,
        in_specs=[IN_HBM],
        out_specs=[IN_VMEM] * 3,
        out_shape=[pltpu.VMEM(state.shape, jnp.float32), edge, edge],
        scratch_shapes=[pltpu.SemaphoreType.DMA((chunks,))],
        compiler_params=params(4),
        name="pack_edges",
    )(state)


def send_sums_kernel(base, period, state_ref, mate_ref, *out_refs):
    inst, _, _, cells = state_ref.shape
    parity = lax.axis_index("inst") % 2
    coefs = [row_coefs(j, inst, period, base, parity) for j in range(inst)]

    def body(cols, _):
        for group, out_ref in zip(SUM_GROUPS, out_refs):
            for n, v in enumerate(group):
                values = [centred(ref[k, v, :, cols], v) for ref in (state_ref, mate_ref) for k in range(inst)]
                sums = [weighted(coefs[j], values) for j in range(inst)]
                out_ref[n, :, cols] = jnp.concatenate(sums, axis=0).astype(jnp.bfloat16)

    columns(cells, LANES, body)


def send_sums(state, mate, base, period):
    inst, _, rows, cells = state.shape
    return pl.pallas_call(
        functools.partial(send_sums_kernel, base, period),
        in_specs=[IN_VMEM] * 2,
        out_specs=[IN_VMEM] * len(SUM_GROUPS),
        out_shape=[pltpu.VMEM((len(g), inst * rows, cells), jnp.bfloat16) for g in SUM_GROUPS],
        compiler_params=params(4),
        name="send_sums",
    )(state, mate)


def expand_blocks(blocks_ref, wide_ref):
    kinds, size, _ = blocks_ref.shape
    nvar = size // TILE
    left = lax.broadcasted_iota(jnp.int32, (TILE, LANES), 1) < TILE
    for kind in range(kinds):
        for a in range(nvar):
            rows = pl.ds(a * TILE, TILE)
            for b in range(nvar):
                lo = (b // 2) * LANES
                hi = min(lo + LANES, size)
                piece = blocks_ref[kind, rows, lo:hi].astype(jnp.float32)
                if hi - lo < LANES:
                    piece = jnp.concatenate([piece, jnp.zeros_like(piece)], axis=1)
                turned = pltpu.roll(piece, TILE, 1)
                first, second = (piece, turned) if b % 2 == 0 else (turned, piece)
                at = pl.ds((kind * nvar + b) * LANES, LANES)
                wide_ref[pl.ds(a * LANES, TILE), at] = jnp.where(left, first, 0.0).astype(jnp.bfloat16)
                wide_ref[pl.ds(a * LANES + TILE, TILE), at] = jnp.where(left, 0.0, second).astype(jnp.bfloat16)


def tile_table(index_ref, type_ref, count, rows, per_row):
    slots = index_ref.shape[1]
    index = index_ref[...]
    slot = lax.broadcasted_iota(jnp.int32, (1, slots), 1)
    code = jnp.where(slot < count, type_ref[...] + 1, 0)
    row_of = lax.broadcasted_iota(jnp.int32, (rows, slots), 0)
    by_row = jnp.where(index // per_row == row_of, code, 0).astype(jnp.float32)
    col_of = lax.broadcasted_iota(jnp.int32, (per_row, slots), 0)
    by_col = jnp.where(index % per_row == col_of, 1.0, 0.0).astype(jnp.float32)
    return lax.dot_general(by_row, by_col, (((1,), (1,)), ((), ())), preferred_element_type=jnp.float32)


def cut_kernel(width, state_ref, blocks_ref, index_ref, type_ref, count_ref, out_ref, wide_ref, lhs_ref):
    inst, nvar, rows, cells = state_ref.shape
    kinds = blocks_ref.shape[0]
    per_row = cells // TILE
    per = inst * rows
    expand_blocks(blocks_ref, wide_ref)
    table = tile_table(index_ref, type_ref, count_ref[lax.axis_index("brick")], rows, per_row)

    def body(cols, chunk):
        tile_at = lax.broadcasted_iota(jnp.int32, (per_row, width), 0)
        cell_at = lax.broadcasted_iota(jnp.int32, (per_row, width), 1) + chunk * width
        spread = jnp.where(cell_at // TILE == tile_at, 1.0, 0.0).astype(jnp.float32)
        kind_map = jnp.dot(table, spread, preferred_element_type=jnp.float32)
        for c in range(width // LANES):
            at = pl.ds(pl.multiple_of(cols.start + c * LANES, LANES), LANES)
            here = kind_map[:, c * LANES:(c + 1) * LANES]
            here = jnp.concatenate([here] * inst, axis=0).astype(jnp.bfloat16)
            for v in range(nvar):
                packed = jnp.concatenate([state_ref[k, v, :, at] for k in range(inst)], axis=0).astype(jnp.bfloat16)
                for kind in range(kinds):
                    lhs_ref[pl.ds(c * per, per), pl.ds((kind * nvar + v) * LANES, LANES)] = jnp.where(
                        here == jnp.bfloat16(kind + 1.0), packed, jnp.bfloat16(0.0)
                    )
        prod = lax.dot_general(
            lhs_ref[...], wide_ref[...], (((1,), (1,)), ((), ())), preferred_element_type=jnp.float32
        )
        for c in range(width // LANES):
            at = pl.ds(pl.multiple_of(cols.start + c * LANES, LANES), LANES)
            for j in range(inst):
                for v in range(nvar):
                    r0 = c * per + j * rows
                    out_ref[j, v, :, at] = prod[r0:r0 + rows, v * LANES:(v + 1) * LANES]

    columns(cells, width, body)


def cut_terms(state, blocks, index, types, counts, width=1024):
    inst, _, rows, _ = state.shape
    kinds, size, _ = blocks.shape
    return pl.pallas_call(
        functools.partial(cut_kernel, width),
        in_specs=[IN_VMEM] * 4 + [IN_SMEM],
        out_specs=IN_VMEM,
        out_shape=pltpu.VMEM(state.shape, jnp.float32),
        scratch_shapes=[
            pltpu.VMEM((2 * size, 2 * size * kinds), jnp.bfloat16),
            pltpu.VMEM((width // LANES * inst * rows, 2 * size * kinds), jnp.bfloat16),
        ],
        compiler_params=params(16),
        name="cut_terms",
    )(state, blocks, index, types, counts)


def flux_of(q):
    inv = 1.0 / jnp.where(q[0] == 0.0, 1.0, q[0])
    speed = q[1] * inv
    press = GAMMA_MINUS * (q[4] - 0.5 * (q[1] * q[1] + q[2] * q[2] + q[3] * q[3]) * inv)
    return [q[1], q[1] * speed + press, q[2] * speed, q[3] * speed, (q[4] + press) * speed]


def turn(x, shift):
    shift = shift % x.shape[0]
    return pltpu.roll(x, shift, 0) if shift else x


def stencil_kernel(period, state_ref, mate_ref, cut_ref, first_ref, second_ref, out_ref):
    inst, nvar, rows, cells = state_ref.shape
    parity = lax.axis_index("inst") % 2
    odd = lax.axis_index("brick") % 2 == 1
    coefs = [row_coefs(j, inst, period, 0, parity) for j in range(inst)]
    row = lax.broadcasted_iota(jnp.int32, (rows, LANES), 0)

    def body(cols, _):
        times, above, below = [], [], []
        for v in range(nvar):
            values = [centred(ref[k, v, :, cols], v) for ref in (state_ref, mate_ref) for k in range(inst)]
            times.append([weighted(coefs[j], values) for j in range(inst)])
            first = first_ref[v, :, cols].astype(jnp.float32)
            second = second_ref[v, :, cols].astype(jnp.float32)
            above.append(jnp.where(odd, second, first))
            below.append(jnp.where(odd, first, second))
        for j in range(inst):
            up, down, smooth = [], [], []
            for v in range(nvar):
                x = state_ref[j, v, :, cols]
                h = jnp.where(row < rows // 2, turn(above[v], -2 * j), turn(below[v], rows - 2 - 2 * j))
                one = turn(jnp.where(row < 1, h, x), -1)
                two = turn(jnp.where(row < 2, h, x), -2)
                back = turn(jnp.where(row >= rows - 1, h, x), 1)
                back2 = turn(jnp.where(row >= rows - 2, h, x), 2)
                up.append(one)
                down.append(back)
                smooth.append(EPS_FOURTH * ((two + back2) - 4.0 * (one + back) + 6.0 * x))
            fup, fdown = flux_of(up), flux_of(down)
            for v in range(nvar):
                total = 0.5 * (fup[v] - fdown[v]) + smooth[v] + times[v][j]
                out_ref[j, v, :, cols] = total + cut_ref[j, v, :, cols]

    columns(cells, LANES, body)


def stencil(state, mate, cut, first, second, period):
    return pl.pallas_call(
        functools.partial(stencil_kernel, period),
        in_specs=[IN_VMEM] * 5,
        out_specs=IN_VMEM,
        out_shape=pltpu.VMEM(state.shape, jnp.float32),
        compiler_params=params(4),
        name="stencil",
    )(state, mate, cut, first, second)


def finish_kernel(variables, sources, period, chunks, part_ref, state_ref, step_ref, *refs):
    inst, _, rows, cells = state_ref.shape
    got_refs = refs[:sources]
    res_ref, new_ref, res_held, new_held, sems = refs[-5:]
    parity = lax.axis_index("inst") % 2
    width = cells // chunks
    copies = []
    for c in range(chunks):
        for n, v in enumerate(variables):

            def body(cols, _, base=c * width, n=n, v=v):
                at = pl.ds(pl.multiple_of(base + cols.start, LANES), LANES)
                if v in STATE_VARS:
                    totals = [part_ref[j, v, :, at] for j in range(inst)]
                    for q in range(sources // 2):
                        coefs = [row_coefs(j, inst, period, 2 * (q + 1), parity) for j in range(inst)]
                        rows_of = [ref[n, :, at].astype(jnp.float32) for ref in got_refs[2 * q:2 * q + 2]]
                        values = [x[k * rows:(k + 1) * rows] for x in rows_of for k in range(inst)]
                        totals = [t + weighted(cf, values) for t, cf in zip(totals, coefs)]
                else:
                    got = [ref[n, :, at].astype(jnp.float32) for ref in got_refs]
                    totals = []
                    for j in range(inst):
                        total = part_ref[j, v, :, at]
                        for g in got:
                            total = total + g[j * rows:(j + 1) * rows]
                        totals.append(total)
                for j in range(inst):
                    res_held[j, n, :, at] = totals[j]
                    new_held[j, n, :, at] = state_ref[j, v, :, at] - step_ref[:, at] * totals[j]

            columns(width, LANES, body)
            cols = pl.ds(c * width, width)
            for held, out, which in ((res_held, res_ref, 0), (new_held, new_ref, 1)):
                copies.append(
                    pltpu.make_async_copy(held.at[:, n, :, cols], out.at[:, v, :, cols], sems.at[which, n, c])
                )
                copies[-1].start()
    for copy in copies:
        copy.wait()


def finish(variables, part, state, step, got, outs, period, chunks=2):
    inst, _, rows, cells = state.shape
    n = len(variables)
    operands = [part, state, step, *got]
    specs = [IN_VMEM] * len(operands)
    aliases = {}
    if outs is not None:
        aliases = {len(operands): 0, len(operands) + 1: 1}
        operands += list(outs)
        specs += [IN_HBM] * 2
    return pl.pallas_call(
        functools.partial(finish_kernel, variables, len(got), period, chunks),
        in_specs=specs,
        out_specs=[IN_HBM] * 2,
        out_shape=[jax.ShapeDtypeStruct(state.shape, jnp.float32)] * 2,
        scratch_shapes=[
            pltpu.VMEM((inst, n, rows, cells), jnp.float32),
            pltpu.VMEM((inst, n, rows, cells), jnp.float32),
            pltpu.SemaphoreType.DMA((2, n, chunks)),
        ],
        input_output_aliases=aliases,
        compiler_params=params(6),
        name="finish",
    )(*operands)


def section(state, time_step, blocks, cut_counts, tile_index, tile_type):
    inst = state.shape[0]
    groups = lax.axis_size("inst")
    bricks = lax.axis_size("brick")
    period = inst * groups
    swap = [(i, i ^ 1) for i in range(groups)]
    hops = [[(i, (i + 2 * q) % groups) for i in range(groups)] for q in range(1, groups // 2)]
    state = pltpu.with_memory_space_constraint(state, pltpu.HBM)

    packed = pack_state(state)
    got_state = [lax.ppermute(packed, "inst", hop) for hop in hops]
    mate = pltpu.with_memory_space_constraint(lax.ppermute(state, "inst", swap), pltpu.VMEM)
    held, first, second = pack_edges(state)
    evens = [(b, b + 1) for b in range(0, bricks - 1, 2)]
    odds = [(b, b + 1) for b in range(1, bricks - 1, 2)]
    first = lax.ppermute(first, "brick", evens + [(b, a) for a, b in evens])
    second = lax.ppermute(second, "brick", odds + [(b, a) for a, b in odds])
    got_sums = [[] for _ in SUM_GROUPS]
    for q, hop in enumerate(hops):
        for g, part in enumerate(send_sums(held, mate, 2 * (q + 1), period)):
            got_sums[g].append(lax.ppermute(part, "inst", hop))
    cut = cut_terms(held, blocks, tile_index, tile_type, cut_counts)
    part = stencil(held, mate, cut, first, second, period)
    pairs = []
    for got in got_state:
        pairs += [got, lax.ppermute(got, "inst", swap)]
    outs = finish(STATE_VARS, part, held, time_step, pairs, None, period)
    for g, group in enumerate(SUM_GROUPS):
        outs = finish(group, part, held, time_step, got_sums[g], outs, period)
    return tuple(outs)


def solution(mesh):
    placed = (
        P(("group", "inst"), None, "brick", None),
        P(("group", "brick"), None),
        P(),
        P("group"),
        P(("group", "brick"), None),
        P(("group", "brick"), None),
    )
    return jax.shard_map(
        section,
        mesh=mesh,
        in_specs=placed,
        out_specs=(
            P(("group", "inst"), None, "brick", None),
            P(("group", "inst"), None, "brick", None),
        ),
        check_vma=False,
    )
```

time: 148 us -> 46 us (0.31)
  the two profiles are of different devices: /device:TPU:0 before, /device:TPU:14 now
where the time goes in v1:
time: 46 us; the launch traced here: 45.8 us
  Pallas kernels  25.3 us (55%)
  waiting for transfers between devices  11.8 us (26%)
  starting transfers between devices  7.88 us (17%)
  between operations  0.79 us (2%)
    ppermute x1, waiting for transfers between devices, section(): got_state = [lax.ppermute(packed, 'inst', hop) for hop in hops]  11.8 us
    pallas_call x1, Pallas kernels, cut_terms(): pl.pallas_call(functools.partial(cut_kernel, width), in_specs=[IN_VMEM] *...  11.4 us
    pallas_call x3, Pallas kernels, finish(): pl.pallas_call(functools.partial(finish_kernel, variables, len(got), peri...  5.02 us
    ppermute x1, starting transfers between devices, section(): second = lax.ppermute(second, 'brick', odds + [(b, a) for a, b in odds])  4.6 us
    pallas_call x1, Pallas kernels, stencil(): pl.pallas_call(functools.partial(stencil_kernel, period), in_specs=[IN_VM...  4.39 us
    ppermute x2, starting transfers between devices, section(): got_sums[g].append(lax.ppermute(part, 'inst', hop))  2.16 us
    pallas_call x1, Pallas kernels, pack_edges(): pl.pallas_call(pack_edges_kernel, in_specs=[IN_HBM], out_specs=[IN_VMEM]...  2 us
    pallas_call x1, Pallas kernels, pack_state(): pl.pallas_call(pack_state_kernel, in_specs=[IN_HBM], out_specs=IN_VMEM, o...  1.35 us
  transfers between devices with their start and end apart: 7, of which 1 were waited for; matrix products, arithmetic and copies ran while one was open for 0% of the time, Pallas kernels for 53%

profile of v1, /device:TPU:14, one launch (start us, length us, event | category | flops | bytes accessed | tf_op | source)
XLA Modules:
  0.0 45.8 jit_solution(1030459890289928470)
XLA Ops:
  0.6 0.1 collective-permute-start
  0.7 1.3 %pack_state.1 = bf16[2,32,4096]{2,1,0:T(8,128)(2,1)S(1)} custom-call(f32[4,5,8,4096]{3,2,1,0:T(8,128)} %state_ref.3), custom_call_target="tpu_custom_call" | custom-call | tf_op jit(solution)/shard_map/pack_state/pallas_call | solution.py:90
  2.1 0.6 %collective-permute-start.5 = (bf16[2,32,4096]{2,1,0:T(8,128)(2,1)S(1)}, bf16[2,32,4096]{2,1,0:T(8,128)(2,1)S(1)}, u32[]{:S(2)}, u32[]{:S(2)}) collective-permute-start(bf16[2,32,4096]{2,1,0:T(8,128)(2,1)S(1)} %pack_state.1), channel_id=1, source_target_pairs={{0,8},{4,12},{8,0},{12,4},{1,9},{5,13},{9,1},{13,5},{2,10},{6,14},... | collective-permute-start | bytes 1572872 | tf_op jit(solution)/shard_map/ppermute | solution.py:392
  2.7 2.0 %pack_edges.1 = (f32[4,5,8,4096]{3,2,1,0:T(8,128)S(1)}, bf16[5,8,4096]{2,1,0:T(8,128)(2,1)S(1)}, bf16[5,8,4096]{2,1,0:T(8,128)(2,1)S(1)}) custom-call(f32[4,5,8,4096]{3,2,1,0:T(8,128)} %state_ref.3), custom_call_target="tpu_custom_call" | custom-call | tf_op jit(solution)/shard_map/pack_edges/pallas_call | solution.py:132
  4.7 11.8 %collective-permute-done.5.refs_0_ = bf16[2,32,4096]{2,1,0:T(8,128)(2,1)S(1)} collective-permute-done((bf16[2,32,4096]{2,1,0:T(8,128)(2,1)S(1)}, bf16[2,32,4096]{2,1,0:T(8,128)(2,1)S(1)}, u32[]{:S(2)}, u32[]{:S(2)}) %collective-permute-start.5) | collective-permute-done | bytes 524320 | tf_op jit(solution)/shard_map/ppermute | solution.py:392
  16.4 0.0 collective-permute-start.6
  16.5 0.0 collective-permute-done.mate_ref
  16.5 0.0 copy-start
  16.5 0.0 copy-start.2
  16.5 0.0 copy-start.3
  16.5 0.0 copy-start.4
  16.5 1.2 %send_sums.1 = (bf16[2,32,4096]{2,1,0:T(8,128)(2,1)S(1)}, bf16[1,32,4096]{2,1,0:T(8,128)(2,1)S(1)}) custom-call(f32[4,5,8,4096]{3,2,1,0:T(8,128)S(1)} %get-tuple-element.11.state_ref, f32[4,5,8,4096]{3,2,1,0:T(8,128)S(1)} %collective-permute-done.mate_ref), custom_call_target="tpu_custom_call" | custom-call | tf_op jit(solution)/shard_map/send_sums/pallas_call | solution.py:160
  17.7 0.6 %collective-permute-start.4 = (bf16[2,32,4096]{2,1,0:T(8,128)(2,1)S(1)}, bf16[2,32,4096]{2,1,0:T(8,128)(2,1)S(1)}, u32[]{:S(2)}, u32[]{:S(2)}) collective-permute-start(bf16[2,32,4096]{2,1,0:T(8,128)(2,1)S(1)} %get-tuple-element.15), channel_id=1, source_target_pairs={{0,8},{4,12},{8,0},{12,4},{1,9},{5,13},{9,1},{13,5},{2,10},{6,14},... | collective-permute-start | bytes 1572872 | tf_op jit(solution)/shard_map/ppermute | solution.py:402
  18.3 0.4 collective-permute-start.1
  18.7 4.6 %collective-permute-start.2 = (bf16[5,8,4096]{2,1,0:T(8,128)(2,1)S(1)}, bf16[5,8,4096]{2,1,0:T(8,128)(2,1)S(1)}, u32[]{:S(2)}, u32[]{:S(2)}) collective-permute-start(bf16[5,8,4096]{2,1,0:T(8,128)(2,1)S(1)} %get-tuple-element.13), channel_id=1, source_target_pairs={{1,2},{2,1},{5,6},{6,5},{9,10},{10,9},{13,14},{14,13},{17,18},{18,... | collective-permute-start | bytes 983048 | tf_op jit(solution)/shard_map/ppermute | solution.py:398
  23.3 1.6 %collective-permute-start.3 = (bf16[1,32,4096]{2,1,0:T(8,128)(2,1)S(1)}, bf16[1,32,4096]{2,1,0:T(8,128)(2,1)S(1)}, u32[]{:S(2)}, u32[]{:S(2)}) collective-permute-start(bf16[1,32,4096]{2,1,0:T(8,128)(2,1)S(1)} %get-tuple-element.14), channel_id=1, source_target_pairs={{0,8},{4,12},{8,0},{12,4},{1,9},{5,13},{9,1},{13,5},{2,10},{6,14},... | collective-permute-start | bytes 786440 | tf_op jit(solution)/shard_map/ppermute | solution.py:402
  24.9 0.0 copy-done
  24.9 0.0 copy-done.2
  24.9 0.0 copy-done.3
  24.9 0.0 copy-done.4
  24.9 11.4 %cut_terms.1.cut_ref = f32[4,5,8,4096]{3,2,1,0:T(8,128)S(1)} custom-call(f32[4,5,8,4096]{3,2,1,0:T(8,128)S(1)} %get-tuple-element.11.state_ref, bf16[8,320,320]{2,1,0:T(8,128)(2,1)S(1)} %copy-done, s32[1,256]{1,0:T(1,128)S(1)} %copy-done.2, s32[1,256]{1,0:T(1,128)S(1)} %copy-done.3, s32[4]{0:T(128)S(1)} %copy-done.4), custom_call_target="tpu_custom_call" | custom-call | tf_op jit(solution)/shard_map/cut_terms/pallas_call | solution.py:241
  36.3 0.0 copy-start.1
  36.3 0.0 collective-permute-done.1.first_ref
  36.4 0.0 collective-permute-done.2.second_ref
  36.4 4.4 %stencil.1.part_ref = f32[4,5,8,4096]{3,2,1,0:T(8,128)S(1)} custom-call(f32[4,5,8,4096]{3,2,1,0:T(8,128)S(1)} %get-tuple-element.11.state_ref, f32[4,5,8,4096]{3,2,1,0:T(8,128)S(1)} %collective-permute-done.mate_ref, f32[4,5,8,4096]{3,2,1,0:T(8,128)S(1)} %cut_terms.1.cut_ref, bf16[5,8,4096]{2,1,0:T(8,128)(2,1)S(1)} %collective-permute-done.1.first_ref, ...), custom_call_target="tpu_custom_call" | custom-call | tf_op jit(solution)/shard_map/stencil/pallas_call | solution.py:304
  40.8 0.0 collective-permute-done.6.refs_1_
  40.8 0.0 copy-done.1
  40.8 2.2 %finish.3 = (f32[4,5,8,4096]{3,2,1,0:T(8,128)}, f32[4,5,8,4096]{3,2,1,0:T(8,128)}) custom-call(f32[4,5,8,4096]{3,2,1,0:T(8,128)S(1)} %stencil.1.part_ref, f32[4,5,8,4096]{3,2,1,0:T(8,128)S(1)} %get-tuple-element.11.state_ref, f32[8,4096]{1,0:T(8,128)S(1)} %copy-done.1, bf16[2,32,4096]{2,1,0:T(8,128)(2,1)S(1)} %collective-permute-done.5.refs_0_, ...), custom_call_target="tpu_custom_call" | custom-call | tf_op jit(solution)/shard_map/finish/pallas_call | solution.py:366
  43.0 0.0 collective-permute-done.4.refs_0_
  43.0 1.6 %finish.4 = (f32[4,5,8,4096]{3,2,1,0:T(8,128)}, f32[4,5,8,4096]{3,2,1,0:T(8,128)}) custom-call(f32[4,5,8,4096]{3,2,1,0:T(8,128)S(1)} %stencil.1.part_ref, f32[4,5,8,4096]{3,2,1,0:T(8,128)S(1)} %get-tuple-element.11.state_ref, f32[8,4096]{1,0:T(8,128)S(1)} %copy-done.1, ...), custom_call_target="tpu_custom_call", output_to_operand_aliasing={{0}: (4, {}), {1}: (5, {})} | custom-call | tf_op jit(solution)/shard_map/finish/pallas_call | solution.py:366
  44.6 0.0 collective-permute-done.3.refs_0_
  44.6 1.2 %finish.5 = (f32[4,5,8,4096]{3,2,1,0:T(8,128)}, f32[4,5,8,4096]{3,2,1,0:T(8,128)}) custom-call(f32[4,5,8,4096]{3,2,1,0:T(8,128)S(1)} %stencil.1.part_ref, f32[4,5,8,4096]{3,2,1,0:T(8,128)S(1)} %get-tuple-element.11.state_ref, f32[8,4096]{1,0:T(8,128)S(1)} %copy-done.1, ...), custom_call_target="tpu_custom_call", output_to_operand_aliasing={{0}: (4, {}), {1}: (5, {})} | custom-call | tf_op jit(solution)/shard_map/finish/pallas_call | solution.py:366
Async XLA Ops:
  0.6 15.8 %collective-permute-start = (f32[4,5,8,4096]{3,2,1,0:T(8,128)}, f32[4,5,8,4096]{3,2,1,0:T(8,128)S(1)}, u32[]{:S(2)}, u32[]{:S(2)}) collective-permute-start(f32[4,5,8,4096]{3,2,1,0:T(8,128)} %state_ref.3), channel_id=1, source_target_pairs={{0,4},{4,0},{8,12},{12,8},{1,5},{5,1},{9,13},{13,9},{2,6},{6,2},{1... | collective-permute-start | bytes 7864328 | tf_op jit(solution)/shard_map/ppermute | solution.py:393
  2.1 14.4 %collective-permute-start.5 = (bf16[2,32,4096]{2,1,0:T(8,128)(2,1)S(1)}, bf16[2,32,4096]{2,1,0:T(8,128)(2,1)S(1)}, u32[]{:S(2)}, u32[]{:S(2)}) collective-permute-start(bf16[2,32,4096]{2,1,0:T(8,128)(2,1)S(1)} %pack_state.1), channel_id=1, source_target_pairs={{0,8},{4,12},{8,0},{12,4},{1,9},{5,13},{9,1},{13,5},{2,10},{6,14},... | collective-permute-start | bytes 1572872 | tf_op jit(solution)/shard_map/ppermute | solution.py:392
  16.4 24.3 %collective-permute-start.6 = (bf16[2,32,4096]{2,1,0:T(8,128)(2,1)S(1)}, bf16[2,32,4096]{2,1,0:T(8,128)(2,1)S(1)}, u32[]{:S(2)}, u32[]{:S(2)}) collective-permute-start(bf16[2,32,4096]{2,1,0:T(8,128)(2,1)S(1)} %collective-permute-done.5.refs_0_), channel_id=1, source_target_pairs={{0,4},{4,0},{8,12},{12,8},{1,5},{5,1},{9,13},{13,9},{2,6},{6,2},{1... | collective-permute-start | bytes 1572872 | tf_op jit(solution)/shard_map/ppermute | solution.py:407
  16.5 8.4 %copy-start = (bf16[8,320,320]{2,1,0:T(8,128)(2,1)S(1)}, bf16[8,320,320]{2,1,0:T(8,128)(2,1)}, u32[]{:S(2)}) copy-start(bf16[8,320,320]{2,1,0:T(8,128)(2,1)} %blocks_ref.1) | copy-start | bytes 4915204
  16.5 8.4 %copy-start.2 = (s32[1,256]{1,0:T(1,128)S(1)}, s32[1,256]{1,0:T(1,128)}, u32[]{:S(2)}) copy-start(s32[1,256]{1,0:T(1,128)} %index_ref.1) | copy-start | bytes 3076
  16.5 8.4 %copy-start.3 = (s32[1,256]{1,0:T(1,128)S(1)}, s32[1,256]{1,0:T(1,128)}, u32[]{:S(2)}) copy-start(s32[1,256]{1,0:T(1,128)} %type_ref.1) | copy-start | bytes 3076
  16.5 8.4 %copy-start.4 = (s32[4]{0:T(128)S(1)}, s32[4]{0:T(128)}, u32[]{:S(2)}) copy-start(s32[4]{0:T(128)} %count_ref.1) | copy-start | bytes 52
  17.7 25.3 %collective-permute-start.4 = (bf16[2,32,4096]{2,1,0:T(8,128)(2,1)S(1)}, bf16[2,32,4096]{2,1,0:T(8,128)(2,1)S(1)}, u32[]{:S(2)}, u32[]{:S(2)}) collective-permute-start(bf16[2,32,4096]{2,1,0:T(8,128)(2,1)S(1)} %get-tuple-element.15), channel_id=1, source_target_pairs={{0,8},{4,12},{8,0},{12,4},{1,9},{5,13},{9,1},{13,5},{2,10},{6,14},... | collective-permute-start | bytes 1572872 | tf_op jit(solution)/shard_map/ppermute | solution.py:402
  18.3 18.1 %collective-permute-start.1 = (bf16[5,8,4096]{2,1,0:T(8,128)(2,1)S(1)}, bf16[5,8,4096]{2,1,0:T(8,128)(2,1)S(1)}, u32[]{:S(2)}, u32[]{:S(2)}) collective-permute-start(bf16[5,8,4096]{2,1,0:T(8,128)(2,1)S(1)} %get-tuple-element.12), channel_id=1, source_target_pairs={{0,1},{2,3},{1,0},{3,2},{4,5},{6,7},{5,4},{7,6},{8,9},{10,11},{9,8... | collective-permute-start | bytes 983048 | tf_op jit(solution)/shard_map/ppermute | solution.py:397
  18.7 17.6 %collective-permute-start.2 = (bf16[5,8,4096]{2,1,0:T(8,128)(2,1)S(1)}, bf16[5,8,4096]{2,1,0:T(8,128)(2,1)S(1)}, u32[]{:S(2)}, u32[]{:S(2)}) collective-permute-start(bf16[5,8,4096]{2,1,0:T(8,128)(2,1)S(1)} %get-tuple-element.13), channel_id=1, source_target_pairs={{1,2},{2,1},{5,6},{6,5},{9,10},{10,9},{13,14},{14,13},{17,18},{18,... | collective-permute-start | bytes 983048 | tf_op jit(solution)/shard_map/ppermute | solution.py:398
  23.3 21.3 %collective-permute-start.3 = (bf16[1,32,4096]{2,1,0:T(8,128)(2,1)S(1)}, bf16[1,32,4096]{2,1,0:T(8,128)(2,1)S(1)}, u32[]{:S(2)}, u32[]{:S(2)}) collective-permute-start(bf16[1,32,4096]{2,1,0:T(8,128)(2,1)S(1)} %get-tuple-element.14), channel_id=1, source_target_pairs={{0,8},{4,12},{8,0},{12,4},{1,9},{5,13},{9,1},{13,5},{2,10},{6,14},... | collective-permute-start | bytes 786440 | tf_op jit(solution)/shard_map/ppermute | solution.py:402
  36.3 4.4 %copy-start.1 = (f32[8,4096]{1,0:T(8,128)S(1)}, f32[8,4096]{1,0:T(8,128)}, u32[]{:S(2)}) copy-start(f32[8,4096]{1,0:T(8,128)} %step_ref.5) | copy-start | bytes 393220

commit v2 on v1

--- a/solution.py
+++ b/solution.py
@@ -12,6 +12,7 @@
 GAMMA_MINUS = 0.4
 EPS_FOURTH = 0.03125
 LANES = 128
+UNROLL = 2
 MIB = 1 << 20
 CENTRE = (1.25, 0.0, 0.0, 0.0, 2.75)
 STATE_VARS = (1, 2)
@@ -84,7 +85,7 @@
         columns(width, LANES, body)
 
 
-def pack_state(state, chunks=2):
+def pack_state(state, chunks=4):
     inst, _, rows, cells = state.shape
     n = len(STATE_VARS)
     return pl.pallas_call(
@@ -126,7 +127,7 @@
         columns(width, LANES, body)
 
 
-def pack_edges(state, chunks=2):
+def pack_edges(state, chunks=4):
     _, nvar, rows, cells = state.shape
     edge = pltpu.VMEM((nvar, rows, cells), jnp.bfloat16)
     return pl.pallas_call(
@@ -167,87 +168,114 @@
     )(state, mate)
 
 
-def expand_blocks(blocks_ref, wide_ref):
+def padded_size(size):
+    return -(-size // LANES) * LANES
+
+
+def cut_kernel(state_ref, blocks_ref, index_ref, type_ref, count_ref, out_ref, tiles_ref, wide_ref, lhs_ref, back_ref):
+    inst, nvar, rows, cells = state_ref.shape
     kinds, size, _ = blocks_ref.shape
-    nvar = size // TILE
-    left = lax.broadcasted_iota(jnp.int32, (TILE, LANES), 1) < TILE
+    slots = index_ref.shape[1]
+    per_row = cells // TILE
+    wide = padded_size(size)
+    half = cells // LANES * rows
+    left = lax.broadcasted_iota(jnp.int32, (2 * rows, LANES), 1) < TILE
+
+    full = size // LANES * LANES
     for kind in range(kinds):
-        for a in range(nvar):
-            rows = pl.ds(a * TILE, TILE)
-            for b in range(nvar):
-                lo = (b // 2) * LANES
-                hi = min(lo + LANES, size)
-                piece = blocks_ref[kind, rows, lo:hi].astype(jnp.float32)
-                if hi - lo < LANES:
-                    piece = jnp.concatenate([piece, jnp.zeros_like(piece)], axis=1)
-                turned = pltpu.roll(piece, TILE, 1)
-                first, second = (piece, turned) if b % 2 == 0 else (turned, piece)
-                at = pl.ds((kind * nvar + b) * LANES, LANES)
-                wide_ref[pl.ds(a * LANES, TILE), at] = jnp.where(left, first, 0.0).astype(jnp.bfloat16)
-                wide_ref[pl.ds(a * LANES + TILE, TILE), at] = jnp.where(left, 0.0, second).astype(jnp.bfloat16)
-
-
-def tile_table(index_ref, type_ref, count, rows, per_row):
-    slots = index_ref.shape[1]
+        wide_ref[0:size, kind * wide:kind * wide + full] = blocks_ref[kind, :, 0:full]
+        rest = blocks_ref[kind, :, full:size]
+        if size > full:
+            blank = jnp.zeros((size, wide - size), jnp.bfloat16)
+            wide_ref[0:size, kind * wide + full:(kind + 1) * wide] = jnp.concatenate([rest, blank], axis=1)
+    if wide > size:
+        wide_ref[size:wide, :] = jnp.zeros((wide - size, kinds * wide), jnp.bfloat16)
+
+    def gather(cols, c):
+        for i in range(inst):
+            q = []
+            for v in range(nvar):
+                pair = [state_ref[i, v, :, pl.ds(pl.multiple_of(cols.start + n * LANES, LANES), LANES)] for n in range(2)]
+                q.append(jnp.concatenate(pair, axis=0))
+            turned = [pltpu.roll(x, TILE, 1) for x in q]
+            for p in range(wide // LANES):
+                u, w = 2 * p, 2 * p + 1
+                lo = jnp.where(left, q[u], turned[w] if w < nvar else 0.0)
+                hi = jnp.where(left, turned[u], q[w] if w < nvar else 0.0)
+                at = pl.ds(i * wide + p * LANES, LANES)
+                row = pl.multiple_of(c * 2 * rows, 2 * rows)
+                tiles_ref[pl.ds(row, 2 * rows), at] = lo.astype(jnp.bfloat16)
+                tiles_ref[pl.ds(half + row, 2 * rows), at] = hi.astype(jnp.bfloat16)
+
+    columns(cells, 2 * LANES, gather)
+
     index = index_ref[...]
-    slot = lax.broadcasted_iota(jnp.int32, (1, slots), 1)
-    code = jnp.where(slot < count, type_ref[...] + 1, 0)
-    row_of = lax.broadcasted_iota(jnp.int32, (rows, slots), 0)
-    by_row = jnp.where(index // per_row == row_of, code, 0).astype(jnp.float32)
-    col_of = lax.broadcasted_iota(jnp.int32, (per_row, slots), 0)
-    by_col = jnp.where(index % per_row == col_of, 1.0, 0.0).astype(jnp.float32)
-    return lax.dot_general(by_row, by_col, (((1,), (1,)), ((), ())), preferred_element_type=jnp.float32)
-
-
-def cut_kernel(width, state_ref, blocks_ref, index_ref, type_ref, count_ref, out_ref, wide_ref, lhs_ref):
-    inst, nvar, rows, cells = state_ref.shape
-    kinds = blocks_ref.shape[0]
-    per_row = cells // TILE
-    per = inst * rows
-    expand_blocks(blocks_ref, wide_ref)
-    table = tile_table(index_ref, type_ref, count_ref[lax.axis_index("brick")], rows, per_row)
-
-    def body(cols, chunk):
-        tile_at = lax.broadcasted_iota(jnp.int32, (per_row, width), 0)
-        cell_at = lax.broadcasted_iota(jnp.int32, (per_row, width), 1) + chunk * width
-        spread = jnp.where(cell_at // TILE == tile_at, 1.0, 0.0).astype(jnp.float32)
-        kind_map = jnp.dot(table, spread, preferred_element_type=jnp.float32)
-        for c in range(width // LANES):
-            at = pl.ds(pl.multiple_of(cols.start + c * LANES, LANES), LANES)
-            here = kind_map[:, c * LANES:(c + 1) * LANES]
-            here = jnp.concatenate([here] * inst, axis=0).astype(jnp.bfloat16)
+    used = lax.broadcasted_iota(jnp.int32, (1, slots), 1) < count_ref[lax.axis_index("brick")]
+    place = index % 2 * half + index % per_row // 2 * rows + index // per_row
+    place = jnp.where(used, place, -1)
+    code = jnp.where(used, type_ref[...] + 1, 0)
+    both = jnp.concatenate([place, code, jnp.zeros((6, slots), jnp.int32)], axis=0).astype(jnp.float32)
+    upright = jnp.transpose(both)
+    place_of = upright[:, 0:1].astype(jnp.int32)
+    code_of = jnp.broadcast_to(upright[:, 1:2], (slots, LANES)).astype(jnp.bfloat16)
+    pick = jnp.where(lax.broadcasted_iota(jnp.int32, (slots, 2 * half), 1) == place_of, 1.0, 0.0).astype(jnp.bfloat16)
+    give = jnp.where(lax.broadcasted_iota(jnp.int32, (2 * half, slots), 0) == place, 1.0, 0.0).astype(jnp.bfloat16)
+
+    chosen = jnp.dot(pick, tiles_ref[...], preferred_element_type=jnp.float32).astype(jnp.bfloat16)
+    for kind in range(kinds):
+        keep = code_of == jnp.bfloat16(kind + 1.0)
+        for i in range(inst):
+            for p in range(wide // LANES):
+                piece = chosen[:, i * wide + p * LANES:i * wide + (p + 1) * LANES]
+                at = pl.ds(kind * wide + p * LANES, LANES)
+                lhs_ref[pl.ds(i * slots, slots), at] = jnp.where(keep, piece, jnp.bfloat16(0.0))
+    prod = lax.dot_general(
+        lhs_ref[...], wide_ref[...], (((1,), (1,)), ((), ())), preferred_element_type=jnp.float32
+    )
+    high = prod.astype(jnp.bfloat16)
+    low = (prod - high.astype(jnp.float32)).astype(jnp.bfloat16)
+    for i in range(inst):
+        at = pl.ds(i * wide, wide)
+        tiles_ref[0:slots, at] = high[i * slots:(i + 1) * slots]
+        tiles_ref[slots:2 * slots, at] = low[i * slots:(i + 1) * slots]
+    give = jnp.concatenate([give, give], axis=1)
+    back_ref[...] = jnp.dot(give, tiles_ref[0:2 * slots, :], preferred_element_type=jnp.float32)
+
+    def scatter(cols, c):
+        row = pl.multiple_of(c * rows, rows)
+        first = lax.broadcasted_iota(jnp.int32, (rows, LANES), 1) < TILE
+        for i in range(inst):
             for v in range(nvar):
-                packed = jnp.concatenate([state_ref[k, v, :, at] for k in range(inst)], axis=0).astype(jnp.bfloat16)
-                for kind in range(kinds):
-                    lhs_ref[pl.ds(c * per, per), pl.ds((kind * nvar + v) * LANES, LANES)] = jnp.where(
-                        here == jnp.bfloat16(kind + 1.0), packed, jnp.bfloat16(0.0)
-                    )
-        prod = lax.dot_general(
-            lhs_ref[...], wide_ref[...], (((1,), (1,)), ((), ())), preferred_element_type=jnp.float32
-        )
-        for c in range(width // LANES):
-            at = pl.ds(pl.multiple_of(cols.start + c * LANES, LANES), LANES)
-            for j in range(inst):
-                for v in range(nvar):
-                    r0 = c * per + j * rows
-                    out_ref[j, v, :, at] = prod[r0:r0 + rows, v * LANES:(v + 1) * LANES]
-
-    columns(cells, width, body)
-
-
-def cut_terms(state, blocks, index, types, counts, width=1024):
-    inst, _, rows, _ = state.shape
+                at = pl.ds(i * wide + v // 2 * LANES, LANES)
+                lo = back_ref[pl.ds(row, rows), at]
+                hi = back_ref[pl.ds(half + row, rows), at]
+                if v % 2 == 0:
+                    hi = pltpu.roll(hi, TILE, 1)
+                else:
+                    lo = pltpu.roll(lo, TILE, 1)
+                out_ref[i, v, :, cols] = jnp.where(first, lo, hi)
+
+    columns(cells, LANES, scatter)
+
+
+def cut_terms(state, blocks, index, types, counts):
+    inst, _, rows, cells = state.shape
     kinds, size, _ = blocks.shape
-    return pl.pallas_call(
-        functools.partial(cut_kernel, width),
+    slots = index.shape[1]
+    wide = padded_size(size)
+    tiles = cells // TILE * rows
+    return pl.pallas_call(
+        cut_kernel,
         in_specs=[IN_VMEM] * 4 + [IN_SMEM],
         out_specs=IN_VMEM,
         out_shape=pltpu.VMEM(state.shape, jnp.float32),
         scratch_shapes=[
-            pltpu.VMEM((2 * size, 2 * size * kinds), jnp.bfloat16),
-            pltpu.VMEM((width // LANES * inst * rows, 2 * size * kinds), jnp.bfloat16),
+            pltpu.VMEM((max(tiles, 2 * slots), inst * wide), jnp.bfloat16),
+            pltpu.VMEM((wide, kinds * wide), jnp.bfloat16),
+            pltpu.VMEM((inst * slots, kinds * wide), jnp.bfloat16),
+            pltpu.VMEM((tiles, inst * wide), jnp.float32),
         ],
-        compiler_params=params(16),
+        compiler_params=params(24),
         name="cut_terms",
     )(state, blocks, index, types, counts)
 
@@ -318,31 +346,36 @@
     parity = lax.axis_index("inst") % 2
     width = cells // chunks
     copies = []
+
+    def one_column(n, v, at):
+        if v in STATE_VARS:
+            totals = [part_ref[j, v, :, at] for j in range(inst)]
+            for q in range(sources // 2):
+                coefs = [row_coefs(j, inst, period, 2 * (q + 1), parity) for j in range(inst)]
+                rows_of = [ref[n, :, at].astype(jnp.float32) for ref in got_refs[2 * q:2 * q + 2]]
+                values = [x[k * rows:(k + 1) * rows] for x in rows_of for k in range(inst)]
+                totals = [t + weighted(cf, values) for t, cf in zip(totals, coefs)]
+        else:
+            got = [ref[n, :, at].astype(jnp.float32) for ref in got_refs]
+            totals = []
+            for j in range(inst):
+                total = part_ref[j, v, :, at]
+                for g in got:
+                    total = total + g[j * rows:(j + 1) * rows]
+                totals.append(total)
+        for j in range(inst):
+            res_held[j, n, :, at] = totals[j]
+            new_held[j, n, :, at] = state_ref[j, v, :, at] - step_ref[:, at] * totals[j]
+
     for c in range(chunks):
         for n, v in enumerate(variables):
 
             def body(cols, _, base=c * width, n=n, v=v):
-                at = pl.ds(pl.multiple_of(base + cols.start, LANES), LANES)
-                if v in STATE_VARS:
-                    totals = [part_ref[j, v, :, at] for j in range(inst)]
-                    for q in range(sources // 2):
-                        coefs = [row_coefs(j, inst, period, 2 * (q + 1), parity) for j in range(inst)]
-                        rows_of = [ref[n, :, at].astype(jnp.float32) for ref in got_refs[2 * q:2 * q + 2]]
-                        values = [x[k * rows:(k + 1) * rows] for x in rows_of for k in range(inst)]
-                        totals = [t + weighted(cf, values) for t, cf in zip(totals, coefs)]
-                else:
-                    got = [ref[n, :, at].astype(jnp.float32) for ref in got_refs]
-                    totals = []
-                    for j in range(inst):
-                        total = part_ref[j, v, :, at]
-                        for g in got:
-                            total = total + g[j * rows:(j + 1) * rows]
-                        totals.append(total)
-                for j in range(inst):
-                    res_held[j, n, :, at] = totals[j]
-                    new_held[j, n, :, at] = state_ref[j, v, :, at] - step_ref[:, at] * totals[j]
-
-            columns(width, LANES, body)
+                for piece in range(UNROLL):
+                    start = base + cols.start + piece * LANES
+                    one_column(n, v, pl.ds(pl.multiple_of(start, LANES), LANES))
+
+            columns(width, UNROLL * LANES, body)
             cols = pl.ds(c * width, width)
             for held, out, which in ((res_held, res_ref, 0), (new_held, new_ref, 1)):
                 copies.append(
@@ -353,7 +386,7 @@
         copy.wait()
 
 
-def finish(variables, part, state, step, got, outs, period, chunks=2):
+def finish(variables, part, state, step, got, outs, period, chunks=4):
     inst, _, rows, cells = state.shape
     n = len(variables)
     operands = [part, state, step, *got]
@@ -390,8 +423,8 @@
 
     packed = pack_state(state)
     got_state = [lax.ppermute(packed, "inst", hop) for hop in hops]
-    mate = pltpu.with_memory_space_constraint(lax.ppermute(state, "inst", swap), pltpu.VMEM)
     held, first, second = pack_edges(state)
+    mate = pltpu.with_memory_space_constraint(lax.ppermute(held, "inst", swap), pltpu.VMEM)
     evens = [(b, b + 1) for b in range(0, bricks - 1, 2)]
     odds = [(b, b + 1) for b in range(1, bricks - 1, 2)]
     first = lax.ppermute(first, "brick", evens + [(b, a) for a, b in evens])

time: 46 us -> 46.3 us (level)
  the two profiles are of different devices: /device:TPU:14 before, /device:TPU:12 now
where the time goes in v2:
time: 46.3 us; the launch traced here: 46.1 us
  Pallas kernels  23.6 us (51%)
  waiting for transfers between devices  12.8 us (28%)
  starting transfers between devices  8.84 us (19%)
  between operations  0.79 us (2%)
    ppermute x1, waiting for transfers between devices, section(): got_state = [lax.ppermute(packed, 'inst', hop) for hop in hops]  12.8 us
    pallas_call x1, Pallas kernels, cut_terms(): pl.pallas_call(cut_kernel, in_specs=[IN_VMEM] * 4 + [IN_SMEM], out_specs=...  10.4 us
    ppermute x1, starting transfers between devices, section(): second = lax.ppermute(second, 'brick', odds + [(b, a) for a, b in odds])  4.6 us
    pallas_call x3, Pallas kernels, finish(): pl.pallas_call(functools.partial(finish_kernel, variables, len(got), peri...  4.49 us
    pallas_call x1, Pallas kernels, stencil(): pl.pallas_call(functools.partial(stencil_kernel, period), in_specs=[IN_VM...  4.39 us
    ppermute x2, starting transfers between devices, section(): got_sums[g].append(lax.ppermute(part, 'inst', hop))  2.16 us
    pallas_call x1, Pallas kernels, pack_edges(): pl.pallas_call(pack_edges_kernel, in_specs=[IN_HBM], out_specs=[IN_VMEM]...  1.85 us
    ppermute x1, starting transfers between devices, section(): got_state = [lax.ppermute(packed, 'inst', hop) for hop in hops]  1.56 us
  transfers between devices with their start and end apart: 7, of which 1 were waited for; matrix products, arithmetic and copies ran while one was open for 0% of the time, Pallas kernels for 45%

profile of v2, /device:TPU:12, one launch (start us, length us, event | category | flops | bytes accessed | tf_op | source)
XLA Modules:
  0.0 46.1 jit_solution(15219888968113289948)
XLA Ops:
  0.6 1.9 %pack_edges.1 = (f32[4,5,8,4096]{3,2,1,0:T(8,128)S(1)}, bf16[5,8,4096]{2,1,0:T(8,128)(2,1)S(1)}, bf16[5,8,4096]{2,1,0:T(8,128)(2,1)S(1)}) custom-call(f32[4,5,8,4096]{3,2,1,0:T(8,128)} %state_ref.3), custom_call_target="tpu_custom_call" | custom-call | tf_op jit(solution)/shard_map/pack_edges/pallas_call | solution.py:133
  2.5 0.1 collective-permute-start
  2.6 1.3 %pack_state.1 = bf16[2,32,4096]{2,1,0:T(8,128)(2,1)S(1)} custom-call(f32[4,5,8,4096]{3,2,1,0:T(8,128)} %state_ref.3), custom_call_target="tpu_custom_call" | custom-call | tf_op jit(solution)/shard_map/pack_state/pallas_call | solution.py:91
  3.9 0.0 copy-start
  3.9 0.0 copy-start.2
  3.9 0.0 copy-start.3
  3.9 0.0 copy-start.4
  3.9 1.6 %collective-permute-start.5 = (bf16[2,32,4096]{2,1,0:T(8,128)(2,1)S(1)}, bf16[2,32,4096]{2,1,0:T(8,128)(2,1)S(1)}, u32[]{:S(2)}, u32[]{:S(2)}) collective-permute-start(bf16[2,32,4096]{2,1,0:T(8,128)(2,1)S(1)} %pack_state.1), channel_id=1, source_target_pairs={{0,8},{4,12},{8,0},{12,4},{1,9},{5,13},{9,1},{13,5},{2,10},{6,14},... | collective-permute-start | bytes 1572872 | tf_op jit(solution)/shard_map/ppermute | solution.py:425
  5.5 12.8 %collective-permute-done.5.refs_0_ = bf16[2,32,4096]{2,1,0:T(8,128)(2,1)S(1)} collective-permute-done((bf16[2,32,4096]{2,1,0:T(8,128)(2,1)S(1)}, bf16[2,32,4096]{2,1,0:T(8,128)(2,1)S(1)}, u32[]{:S(2)}, u32[]{:S(2)}) %collective-permute-start.5) | collective-permute-done | bytes 524320 | tf_op jit(solution)/shard_map/ppermute | solution.py:425
  18.3 0.0 collective-permute-start.6
  18.3 0.0 collective-permute-done.mate_ref
  18.3 1.1 %send_sums.1 = (bf16[2,32,4096]{2,1,0:T(8,128)(2,1)S(1)}, bf16[1,32,4096]{2,1,0:T(8,128)(2,1)S(1)}) custom-call(f32[4,5,8,4096]{3,2,1,0:T(8,128)S(1)} %get-tuple-element.11.state_ref, f32[4,5,8,4096]{3,2,1,0:T(8,128)S(1)} %collective-permute-done.mate_ref), custom_call_target="tpu_custom_call" | custom-call | tf_op jit(solution)/shard_map/send_sums/pallas_call | solution.py:161
  19.5 1.6 %collective-permute-start.4 = (bf16[2,32,4096]{2,1,0:T(8,128)(2,1)S(1)}, bf16[2,32,4096]{2,1,0:T(8,128)(2,1)S(1)}, u32[]{:S(2)}, u32[]{:S(2)}) collective-permute-start(bf16[2,32,4096]{2,1,0:T(8,128)(2,1)S(1)} %get-tuple-element.15), channel_id=1, source_target_pairs={{0,8},{4,12},{8,0},{12,4},{1,9},{5,13},{9,1},{13,5},{2,10},{6,14},... | collective-permute-start | bytes 1572872 | tf_op jit(solution)/shard_map/ppermute | solution.py:435
  21.0 0.4 collective-permute-start.1
  21.5 4.6 %collective-permute-start.2 = (bf16[5,8,4096]{2,1,0:T(8,128)(2,1)S(1)}, bf16[5,8,4096]{2,1,0:T(8,128)(2,1)S(1)}, u32[]{:S(2)}, u32[]{:S(2)}) collective-permute-start(bf16[5,8,4096]{2,1,0:T(8,128)(2,1)S(1)} %get-tuple-element.13), channel_id=1, source_target_pairs={{1,2},{2,1},{5,6},{6,5},{9,10},{10,9},{13,14},{14,13},{17,18},{18,... | collective-permute-start | bytes 983048 | tf_op jit(solution)/shard_map/ppermute | solution.py:431
  26.1 0.6 %collective-permute-start.3 = (bf16[1,32,4096]{2,1,0:T(8,128)(2,1)S(1)}, bf16[1,32,4096]{2,1,0:T(8,128)(2,1)S(1)}, u32[]{:S(2)}, u32[]{:S(2)}) collective-permute-start(bf16[1,32,4096]{2,1,0:T(8,128)(2,1)S(1)} %get-tuple-element.14), channel_id=1, source_target_pairs={{0,8},{4,12},{8,0},{12,4},{1,9},{5,13},{9,1},{13,5},{2,10},{6,14},... | collective-permute-start | bytes 786440 | tf_op jit(solution)/shard_map/ppermute | solution.py:435
  26.7 0.0 copy-done
  26.7 0.0 copy-done.2
  26.7 0.0 copy-done.3
  26.7 0.0 copy-done.4
  26.7 10.4 %cut_terms.1.cut_ref = f32[4,5,8,4096]{3,2,1,0:T(8,128)S(1)} custom-call(f32[4,5,8,4096]{3,2,1,0:T(8,128)S(1)} %get-tuple-element.11.state_ref, bf16[8,320,320]{2,1,0:T(8,128)(2,1)S(1)} %copy-done, s32[1,256]{1,0:T(1,128)S(1)} %copy-done.2, s32[1,256]{1,0:T(1,128)S(1)} %copy-done.3, s32[4]{0:T(128)S(1)} %copy-done.4), custom_call_target="tpu_custom_call" | custom-call | tf_op jit(solution)/shard_map/cut_terms/pallas_call | solution.py:267
  37.1 0.0 copy-start.1
  37.1 0.0 collective-permute-done.1.first_ref
  37.2 0.0 collective-permute-done.2.second_ref
  37.2 4.4 %stencil.1.part_ref = f32[4,5,8,4096]{3,2,1,0:T(8,128)S(1)} custom-call(f32[4,5,8,4096]{3,2,1,0:T(8,128)S(1)} %get-tuple-element.11.state_ref, f32[4,5,8,4096]{3,2,1,0:T(8,128)S(1)} %collective-permute-done.mate_ref, f32[4,5,8,4096]{3,2,1,0:T(8,128)S(1)} %cut_terms.1.cut_ref, bf16[5,8,4096]{2,1,0:T(8,128)(2,1)S(1)} %collective-permute-done.1.first_ref, ...), custom_call_target="tpu_custom_call" | custom-call | tf_op jit(solution)/shard_map/stencil/pallas_call | solution.py:332
  41.6 0.0 collective-permute-done.6.refs_1_
  41.6 0.0 copy-done.1
  41.6 1.9 %finish.3 = (f32[4,5,8,4096]{3,2,1,0:T(8,128)}, f32[4,5,8,4096]{3,2,1,0:T(8,128)}) custom-call(f32[4,5,8,4096]{3,2,1,0:T(8,128)S(1)} %stencil.1.part_ref, f32[4,5,8,4096]{3,2,1,0:T(8,128)S(1)} %get-tuple-element.11.state_ref, f32[8,4096]{1,0:T(8,128)S(1)} %copy-done.1, bf16[2,32,4096]{2,1,0:T(8,128)(2,1)S(1)} %collective-permute-done.5.refs_0_, ...), custom_call_target="tpu_custom_call" | custom-call | tf_op jit(solution)/shard_map/finish/pallas_call | solution.py:399
  43.5 0.0 collective-permute-done.4.refs_0_
  43.5 1.5 %finish.4 = (f32[4,5,8,4096]{3,2,1,0:T(8,128)}, f32[4,5,8,4096]{3,2,1,0:T(8,128)}) custom-call(f32[4,5,8,4096]{3,2,1,0:T(8,128)S(1)} %stencil.1.part_ref, f32[4,5,8,4096]{3,2,1,0:T(8,128)S(1)} %get-tuple-element.11.state_ref, f32[8,4096]{1,0:T(8,128)S(1)} %copy-done.1, ...), custom_call_target="tpu_custom_call", output_to_operand_aliasing={{0}: (4, {}), {1}: (5, {})} | custom-call | tf_op jit(solution)/shard_map/finish/pallas_call | solution.py:399
  45.0 0.0 collective-permute-done.3.refs_0_
  45.0 1.1 %finish.5 = (f32[4,5,8,4096]{3,2,1,0:T(8,128)}, f32[4,5,8,4096]{3,2,1,0:T(8,128)}) custom-call(f32[4,5,8,4096]{3,2,1,0:T(8,128)S(1)} %stencil.1.part_ref, f32[4,5,8,4096]{3,2,1,0:T(8,128)S(1)} %get-tuple-element.11.state_ref, f32[8,4096]{1,0:T(8,128)S(1)} %copy-done.1, ...), custom_call_target="tpu_custom_call", output_to_operand_aliasing={{0}: (4, {}), {1}: (5, {})} | custom-call | tf_op jit(solution)/shard_map/finish/pallas_call | solution.py:399
Async XLA Ops:
  2.5 15.8 %collective-permute-start = (f32[4,5,8,4096]{3,2,1,0:T(8,128)S(1)}, f32[4,5,8,4096]{3,2,1,0:T(8,128)S(1)}, u32[]{:S(2)}, u32[]{:S(2)}) collective-permute-start(f32[4,5,8,4096]{3,2,1,0:T(8,128)S(1)} %get-tuple-element.11.state_ref), channel_id=1, source_target_pairs={{0,4},{4,0},{8,12},{12,8},{1,5},{5,1},{9,13},{13,9},{2,6},{6,2},{1... | collective-permute-start | bytes 7864328 | tf_op jit(solution)/shard_map/ppermute | solution.py:427
  3.9 22.8 %copy-start = (bf16[8,320,320]{2,1,0:T(8,128)(2,1)S(1)}, bf16[8,320,320]{2,1,0:T(8,128)(2,1)}, u32[]{:S(2)}) copy-start(bf16[8,320,320]{2,1,0:T(8,128)(2,1)} %blocks_ref.1) | copy-start | bytes 4915204
  3.9 22.8 %copy-start.2 = (s32[1,256]{1,0:T(1,128)S(1)}, s32[1,256]{1,0:T(1,128)}, u32[]{:S(2)}) copy-start(s32[1,256]{1,0:T(1,128)} %index_ref.1) | copy-start | bytes 3076
  3.9 22.8 %copy-start.3 = (s32[1,256]{1,0:T(1,128)S(1)}, s32[1,256]{1,0:T(1,128)}, u32[]{:S(2)}) copy-start(s32[1,256]{1,0:T(1,128)} %type_ref.1) | copy-start | bytes 3076
  3.9 22.8 %copy-start.4 = (s32[4]{0:T(128)S(1)}, s32[4]{0:T(128)}, u32[]{:S(2)}) copy-start(s32[4]{0:T(128)} %count_ref.1) | copy-start | bytes 52
  3.9 14.4 %collective-permute-start.5 = (bf16[2,32,4096]{2,1,0:T(8,128)(2,1)S(1)}, bf16[2,32,4096]{2,1,0:T(8,128)(2,1)S(1)}, u32[]{:S(2)}, u32[]{:S(2)}) collective-permute-start(bf16[2,32,4096]{2,1,0:T(8,128)(2,1)S(1)} %pack_state.1), channel_id=1, source_target_pairs={{0,8},{4,12},{8,0},{12,4},{1,9},{5,13},{9,1},{13,5},{2,10},{6,14},... | collective-permute-start | bytes 1572872 | tf_op jit(solution)/shard_map/ppermute | solution.py:425
  18.3 23.3 %collective-permute-start.6 = (bf16[2,32,4096]{2,1,0:T(8,128)(2,1)S(1)}, bf16[2,32,4096]{2,1,0:T(8,128)(2,1)S(1)}, u32[]{:S(2)}, u32[]{:S(2)}) collective-permute-start(bf16[2,32,4096]{2,1,0:T(8,128)(2,1)S(1)} %collective-permute-done.5.refs_0_), channel_id=1, source_target_pairs={{0,4},{4,0},{8,12},{12,8},{1,5},{5,1},{9,13},{13,9},{2,6},{6,2},{1... | collective-permute-start | bytes 1572872 | tf_op jit(solution)/shard_map/ppermute | solution.py:440
  19.5 24.0 %collective-permute-start.4 = (bf16[2,32,4096]{2,1,0:T(8,128)(2,1)S(1)}, bf16[2,32,4096]{2,1,0:T(8,128)(2,1)S(1)}, u32[]{:S(2)}, u32[]{:S(2)}) collective-permute-start(bf16[2,32,4096]{2,1,0:T(8,128)(2,1)S(1)} %get-tuple-element.15), channel_id=1, source_target_pairs={{0,8},{4,12},{8,0},{12,4},{1,9},{5,13},{9,1},{13,5},{2,10},{6,14},... | collective-permute-start | bytes 1572872 | tf_op jit(solution)/shard_map/ppermute | solution.py:435
  21.0 16.1 %collective-permute-start.1 = (bf16[5,8,4096]{2,1,0:T(8,128)(2,1)S(1)}, bf16[5,8,4096]{2,1,0:T(8,128)(2,1)S(1)}, u32[]{:S(2)}, u32[]{:S(2)}) collective-permute-start(bf16[5,8,4096]{2,1,0:T(8,128)(2,1)S(1)} %get-tuple-element.12), channel_id=1, source_target_pairs={{0,1},{2,3},{1,0},{3,2},{4,5},{6,7},{5,4},{7,6},{8,9},{10,11},{9,8... | collective-permute-start | bytes 983048 | tf_op jit(solution)/shard_map/ppermute | solution.py:430
  21.5 15.7 %collective-permute-start.2 = (bf16[5,8,4096]{2,1,0:T(8,128)(2,1)S(1)}, bf16[5,8,4096]{2,1,0:T(8,128)(2,1)S(1)}, u32[]{:S(2)}, u32[]{:S(2)}) collective-permute-start(bf16[5,8,4096]{2,1,0:T(8,128)(2,1)S(1)} %get-tuple-element.13), channel_id=1, source_target_pairs={{1,2},{2,1},{5,6},{6,5},{9,10},{10,9},{13,14},{14,13},{17,18},{18,... | collective-permute-start | bytes 983048 | tf_op jit(solution)/shard_map/ppermute | solution.py:431
  26.1 18.9 %collective-permute-start.3 = (bf16[1,32,4096]{2,1,0:T(8,128)(2,1)S(1)}, bf16[1,32,4096]{2,1,0:T(8,128)(2,1)S(1)}, u32[]{:S(2)}, u32[]{:S(2)}) collective-permute-start(bf16[1,32,4096]{2,1,0:T(8,128)(2,1)S(1)} %get-tuple-element.14), channel_id=1, source_target_pairs={{0,8},{4,12},{8,0},{12,4},{1,9},{5,13},{9,1},{13,5},{2,10},{6,14},... | collective-permute-start | bytes 786440 | tf_op jit(solution)/shard_map/ppermute | solution.py:435
  37.1 4.4 %copy-start.1 = (f32[8,4096]{1,0:T(8,128)S(1)}, f32[8,4096]{1,0:T(8,128)}, u32[]{:S(2)}) copy-start(f32[8,4096]{1,0:T(8,128)} %step_ref.5) | copy-start | bytes 393220

commit v3 on v2

--- a/solution.py
+++ b/solution.py
@@ -15,8 +15,9 @@
 UNROLL = 2
 MIB = 1 << 20
 CENTRE = (1.25, 0.0, 0.0, 0.0, 2.75)
-STATE_VARS = (1, 2)
-SUM_GROUPS = ((3, 4), (0,))
+STATE_GROUPS = ((1, 2),)
+PARTS = 2
+SUM_GROUPS = (((3, 0, 2), (4, 0, 2), (0, 0, 1)), ((0, 1, 2),))
 
 IN_VMEM = pl.BlockSpec(memory_space=pltpu.VMEM)
 IN_HBM = pl.BlockSpec(memory_space=pltpu.HBM)
@@ -63,11 +64,26 @@
     lax.fori_loop(0, cells // width, one, 0)
 
 
-def pack_state_kernel(state_ref, out_ref, held_ref, sems):
+def turn(x, shift):
+    shift = shift % x.shape[0]
+    return pltpu.roll(x, shift, 0) if shift else x
+
+
+def pack_columns(refs_of, variables, inst, out_ref, base, cells):
+    def body(cols, _):
+        at = pl.ds(pl.multiple_of(base + cols.start, LANES), LANES)
+        for n, v in enumerate(variables):
+            packed = jnp.concatenate([centred(refs_of(k, n, at), v) for k in range(inst)], axis=0)
+            out_ref[n, :, at] = packed.astype(jnp.bfloat16)
+
+    columns(cells, LANES, body)
+
+
+def pack_state_kernel(variables, state_ref, out_ref, held_ref, sems):
     inst, _, _, cells = state_ref.shape
     chunks = sems.shape[0]
     width = cells // chunks
-    lo, hi = STATE_VARS[0], STATE_VARS[-1] + 1
+    lo, hi = variables[0], variables[-1] + 1
     copies = []
     for c in range(chunks):
         cols = pl.ds(c * width, width)
@@ -75,21 +91,14 @@
         copies[-1].start()
     for c in range(chunks):
         copies[c].wait()
-
-        def body(cols, _, base=c * width):
-            at = pl.ds(pl.multiple_of(base + cols.start, LANES), LANES)
-            for n, v in enumerate(STATE_VARS):
-                packed = jnp.concatenate([centred(held_ref[k, n, :, at], v) for k in range(inst)], axis=0)
-                out_ref[n, :, at] = packed.astype(jnp.bfloat16)
-
-        columns(width, LANES, body)
-
-
-def pack_state(state, chunks=4):
+        pack_columns(lambda k, n, at: held_ref[k, n, :, at], variables, inst, out_ref, c * width, width)
+
+
+def pack_state(state, variables, chunks=4):
     inst, _, rows, cells = state.shape
-    n = len(STATE_VARS)
-    return pl.pallas_call(
-        pack_state_kernel,
+    n = len(variables)
+    return pl.pallas_call(
+        functools.partial(pack_state_kernel, variables),
         in_specs=[IN_HBM],
         out_specs=IN_VMEM,
         out_shape=pltpu.VMEM((n, inst * rows, cells), jnp.bfloat16),
@@ -99,61 +108,80 @@
     )(state)
 
 
-def pack_edges_kernel(state_ref, held_ref, first_ref, second_ref, sems):
+def pack_more_kernel(variables, state_ref, out_ref):
+    inst, _, _, cells = state_ref.shape
+    pack_columns(lambda k, n, at: state_ref[k, variables[n], :, at], variables, inst, out_ref, 0, cells)
+
+
+def pack_more(state, variables):
+    inst, _, rows, cells = state.shape
+    return pl.pallas_call(
+        functools.partial(pack_more_kernel, variables),
+        in_specs=[IN_VMEM],
+        out_specs=IN_VMEM,
+        out_shape=pltpu.VMEM((len(variables), inst * rows, cells), jnp.bfloat16),
+        compiler_params=params(2),
+        name="pack_more",
+    )(state)
+
+
+def pack_edges_kernel(state_ref, first_ref, second_ref):
     inst, nvar, rows, cells = state_ref.shape
-    chunks = sems.shape[0]
-    width = cells // chunks
     odd = lax.axis_index("brick") % 2 == 1
-    copies = []
-    for c in range(chunks):
-        cols = pl.ds(c * width, width)
-        copies.append(pltpu.make_async_copy(state_ref.at[:, :, :, cols], held_ref.at[:, :, :, cols], sems.at[c]))
-        copies[-1].start()
     pair = lax.broadcasted_iota(jnp.int32, (rows, LANES), 0) // 2
-    for c in range(chunks):
-        copies[c].wait()
-
-        def body(cols, _, base=c * width):
-            at = pl.ds(pl.multiple_of(base + cols.start, LANES), LANES)
-            for v in range(nvar):
-                q = [held_ref[j, v, :, at] for j in range(inst)]
-                head, tail = q[0], pltpu.roll(q[0], 2, 0)
-                for j in range(1, inst):
-                    head = jnp.where(pair == j, pltpu.roll(q[j], 2 * j, 0), head)
-                    tail = jnp.where(pair == j, pltpu.roll(q[j], (2 * j + 2) % rows, 0) if (2 * j + 2) % rows else q[j], tail)
-                first_ref[v, :, at] = jnp.where(odd, head, tail).astype(jnp.bfloat16)
-                second_ref[v, :, at] = jnp.where(odd, tail, head).astype(jnp.bfloat16)
-
-        columns(width, LANES, body)
-
-
-def pack_edges(state, chunks=4):
+
+    def body(cols, _):
+        for v in range(nvar):
+            q = [state_ref[j, v, :, cols] for j in range(inst)]
+            head, tail = q[0], turn(q[0], 2)
+            for j in range(1, inst):
+                head = jnp.where(pair == j, turn(q[j], 2 * j), head)
+                tail = jnp.where(pair == j, turn(q[j], 2 * j + 2), tail)
+            first_ref[v, :, cols] = jnp.where(odd, head, tail).astype(jnp.bfloat16)
+            second_ref[v, :, cols] = jnp.where(odd, tail, head).astype(jnp.bfloat16)
+
+    columns(cells, LANES, body)
+
+
+def pack_edges(state):
     _, nvar, rows, cells = state.shape
     edge = pltpu.VMEM((nvar, rows, cells), jnp.bfloat16)
     return pl.pallas_call(
         pack_edges_kernel,
-        in_specs=[IN_HBM],
-        out_specs=[IN_VMEM] * 3,
-        out_shape=[pltpu.VMEM(state.shape, jnp.float32), edge, edge],
-        scratch_shapes=[pltpu.SemaphoreType.DMA((chunks,))],
-        compiler_params=params(4),
+        in_specs=[IN_VMEM],
+        out_specs=[IN_VMEM] * 2,
+        out_shape=[edge, edge],
+        compiler_params=params(2),
         name="pack_edges",
     )(state)
+
+
+def laid_out(group, cells):
+    pieces, at = [], 0
+    for v, lo, hi in group:
+        count = (hi - lo) * cells // PARTS
+        pieces.append((v, lo * cells // PARTS, count, at))
+        at += count
+    return pieces, at
 
 
 def send_sums_kernel(base, period, state_ref, mate_ref, *out_refs):
     inst, _, _, cells = state_ref.shape
     parity = lax.axis_index("inst") % 2
     coefs = [row_coefs(j, inst, period, base, parity) for j in range(inst)]
-
-    def body(cols, _):
-        for group, out_ref in zip(SUM_GROUPS, out_refs):
-            for n, v in enumerate(group):
-                values = [centred(ref[k, v, :, cols], v) for ref in (state_ref, mate_ref) for k in range(inst)]
-                sums = [weighted(coefs[j], values) for j in range(inst)]
-                out_ref[n, :, cols] = jnp.concatenate(sums, axis=0).astype(jnp.bfloat16)
-
-    columns(cells, LANES, body)
+    for group, out_ref in zip(SUM_GROUPS, out_refs):
+        for v, first, count, to in laid_out(group, cells)[0]:
+
+            def body(cols, _, v=v, first=first, to=to, out_ref=out_ref):
+                for piece in range(UNROLL):
+                    start = cols.start + piece * LANES
+                    src = pl.ds(pl.multiple_of(first + start, LANES), LANES)
+                    dst = pl.ds(pl.multiple_of(to + start, LANES), LANES)
+                    values = [centred(ref[k, v, :, src], v) for ref in (state_ref, mate_ref) for k in range(inst)]
+                    sums = [weighted(coefs[j], values) for j in range(inst)]
+                    out_ref[:, dst] = jnp.concatenate(sums, axis=0).astype(jnp.bfloat16)
+
+            columns(count, UNROLL * LANES, body)
 
 
 def send_sums(state, mate, base, period):
@@ -162,7 +190,7 @@
         functools.partial(send_sums_kernel, base, period),
         in_specs=[IN_VMEM] * 2,
         out_specs=[IN_VMEM] * len(SUM_GROUPS),
-        out_shape=[pltpu.VMEM((len(g), inst * rows, cells), jnp.bfloat16) for g in SUM_GROUPS],
+        out_shape=[pltpu.VMEM((inst * rows, laid_out(g, cells)[1]), jnp.bfloat16) for g in SUM_GROUPS],
         compiler_params=params(4),
         name="send_sums",
     )(state, mate)
@@ -285,11 +313,6 @@
     speed = q[1] * inv
     press = GAMMA_MINUS * (q[4] - 0.5 * (q[1] * q[1] + q[2] * q[2] + q[3] * q[3]) * inv)
     return [q[1], q[1] * speed + press, q[2] * speed, q[3] * speed, (q[4] + press) * speed]
-
-
-def turn(x, shift):
-    shift = shift % x.shape[0]
-    return pltpu.roll(x, shift, 0) if shift else x
 
 
 def stencil_kernel(period, state_ref, mate_ref, cut_ref, first_ref, second_ref, out_ref):
@@ -339,57 +362,59 @@
     )(state, mate, cut, first, second)
 
 
-def finish_kernel(variables, sources, period, chunks, part_ref, state_ref, step_ref, *refs):
-    inst, _, rows, cells = state_ref.shape
-    got_refs = refs[:sources]
+def finish_kernel(groups, period, part_ref, state_ref, step_ref, *refs):
+    inst, _, rows, _ = state_ref.shape
     res_ref, new_ref, res_held, new_held, sems = refs[-5:]
     parity = lax.axis_index("inst") % 2
-    width = cells // chunks
+    jobs, at = [], 0
+    for whole, pieces, count in groups:
+        got_refs = refs[at:at + count]
+        at += count
+        jobs += [(whole, n, v, first, size, to, got_refs) for n, (v, first, size, to) in enumerate(pieces)]
     copies = []
-
-    def one_column(n, v, at):
-        if v in STATE_VARS:
+    for m, (whole, n, v, first, size, to, got_refs) in enumerate(jobs):
+
+        def one_column(start, m=m, whole=whole, n=n, v=v, first=first, to=to, got_refs=got_refs):
+            at = pl.ds(pl.multiple_of(first + start, LANES), LANES)
+            dst = pl.ds(pl.multiple_of(to + start, LANES), LANES)
             totals = [part_ref[j, v, :, at] for j in range(inst)]
-            for q in range(sources // 2):
-                coefs = [row_coefs(j, inst, period, 2 * (q + 1), parity) for j in range(inst)]
-                rows_of = [ref[n, :, at].astype(jnp.float32) for ref in got_refs[2 * q:2 * q + 2]]
-                values = [x[k * rows:(k + 1) * rows] for x in rows_of for k in range(inst)]
-                totals = [t + weighted(cf, values) for t, cf in zip(totals, coefs)]
-        else:
-            got = [ref[n, :, at].astype(jnp.float32) for ref in got_refs]
-            totals = []
+            if whole:
+                for q in range(len(got_refs) // 2):
+                    coefs = [row_coefs(j, inst, period, 2 * (q + 1), parity) for j in range(inst)]
+                    rows_of = [ref[n, :, at].astype(jnp.float32) for ref in got_refs[2 * q:2 * q + 2]]
+                    values = [x[k * rows:(k + 1) * rows] for x in rows_of for k in range(inst)]
+                    totals = [t + weighted(cf, values) for t, cf in zip(totals, coefs)]
+            else:
+                for ref in got_refs:
+                    g = ref[:, dst].astype(jnp.float32)
+                    totals = [t + g[j * rows:(j + 1) * rows] for j, t in enumerate(totals)]
             for j in range(inst):
-                total = part_ref[j, v, :, at]
-                for g in got:
-                    total = total + g[j * rows:(j + 1) * rows]
-                totals.append(total)
-        for j in range(inst):
-            res_held[j, n, :, at] = totals[j]
-            new_held[j, n, :, at] = state_ref[j, v, :, at] - step_ref[:, at] * totals[j]
-
-    for c in range(chunks):
-        for n, v in enumerate(variables):
-
-            def body(cols, _, base=c * width, n=n, v=v):
+                res_held[j, m, :, at] = totals[j]
+                new_held[j, m, :, at] = state_ref[j, v, :, at] - step_ref[:, at] * totals[j]
+
+        chunks = sems.shape[2]
+        width = size // chunks
+        for c in range(chunks):
+
+            def body(cols, _, base=c * width, one_column=one_column):
                 for piece in range(UNROLL):
-                    start = base + cols.start + piece * LANES
-                    one_column(n, v, pl.ds(pl.multiple_of(start, LANES), LANES))
+                    one_column(base + cols.start + piece * LANES)
 
             columns(width, UNROLL * LANES, body)
-            cols = pl.ds(c * width, width)
+            cols = pl.ds(first + c * width, width)
             for held, out, which in ((res_held, res_ref, 0), (new_held, new_ref, 1)):
                 copies.append(
-                    pltpu.make_async_copy(held.at[:, n, :, cols], out.at[:, v, :, cols], sems.at[which, n, c])
+                    pltpu.make_async_copy(held.at[:, m, :, cols], out.at[:, v, :, cols], sems.at[which, m, c])
                 )
                 copies[-1].start()
     for copy in copies:
         copy.wait()
 
 
-def finish(variables, part, state, step, got, outs, period, chunks=4):
+def finish(groups, part, state, step, outs, period, chunks=2):
     inst, _, rows, cells = state.shape
-    n = len(variables)
-    operands = [part, state, step, *got]
+    n = sum(len(pieces) for _, pieces, _ in groups)
+    operands = [part, state, step] + [x for _, _, got in groups for x in got]
     specs = [IN_VMEM] * len(operands)
     aliases = {}
     if outs is not None:
@@ -397,7 +422,7 @@
         operands += list(outs)
         specs += [IN_HBM] * 2
     return pl.pallas_call(
-        functools.partial(finish_kernel, variables, len(got), period, chunks),
+        functools.partial(finish_kernel, [(w, p, len(got)) for w, p, got in groups], period),
         in_specs=specs,
         out_specs=[IN_HBM] * 2,
         out_shape=[jax.ShapeDtypeStruct(state.shape, jnp.float32)] * 2,
@@ -407,7 +432,7 @@
             pltpu.SemaphoreType.DMA((2, n, chunks)),
         ],
         input_output_aliases=aliases,
-        compiler_params=params(6),
+        compiler_params=params(8),
         name="finish",
     )(*operands)
 
@@ -419,11 +444,12 @@
     period = inst * groups
     swap = [(i, i ^ 1) for i in range(groups)]
     hops = [[(i, (i + 2 * q) % groups) for i in range(groups)] for q in range(1, groups // 2)]
-    state = pltpu.with_memory_space_constraint(state, pltpu.HBM)
-
-    packed = pack_state(state)
-    got_state = [lax.ppermute(packed, "inst", hop) for hop in hops]
-    held, first, second = pack_edges(state)
+    cells = state.shape[3]
+    packed = [pack_state(pltpu.with_memory_space_constraint(state, pltpu.HBM), STATE_GROUPS[0])]
+    held = pltpu.with_memory_space_constraint(state, pltpu.VMEM)
+    packed += [pack_more(held, group) for group in STATE_GROUPS[1:]]
+    got_state = [[lax.ppermute(p, "inst", hop) for hop in hops] for p in packed]
+    first, second = pack_edges(held)
     mate = pltpu.with_memory_space_constraint(lax.ppermute(held, "inst", swap), pltpu.VMEM)
     evens = [(b, b + 1) for b in range(0, bricks - 1, 2)]
     odds = [(b, b + 1) for b in range(1, bricks - 1, 2)]
@@ -435,12 +461,17 @@
             got_sums[g].append(lax.ppermute(part, "inst", hop))
     cut = cut_terms(held, blocks, tile_index, tile_type, cut_counts)
     part = stencil(held, mate, cut, first, second, period)
-    pairs = []
-    for got in got_state:
-        pairs += [got, lax.ppermute(got, "inst", swap)]
-    outs = finish(STATE_VARS, part, held, time_step, pairs, None, period)
-    for g, group in enumerate(SUM_GROUPS):
-        outs = finish(group, part, held, time_step, got_sums[g], outs, period)
+    groups = []
+    for variables, got in zip(STATE_GROUPS, got_state):
+        pairs = []
+        for x in got:
+            pairs += [x, lax.ppermute(x, "inst", swap)]
+        groups.append((True, [(v, 0, cells, 0) for v in variables], pairs))
+    steps = [groups]
+    steps += [[(False, laid_out(group, cells)[0], got)] for group, got in zip(SUM_GROUPS, got_sums)]
+    outs = None
+    for step in steps:
+        outs = finish(step, part, held, time_step, outs, period)
     return tuple(outs)
 
 

time: 46.3 us -> 43.9 us (0.948)
  waiting for transfers between devices: 12.8 us -> 10.4 us
  starting transfers between devices: 8.84 us -> 9.86 us
  Pallas kernels: 23.6 us -> 22.6 us
    ppermute x2, waiting for transfers between devices: 12.8 us -> 8.27 us  [the longest x1 8.27 us: section(): got_state = [[lax.ppermute(p, 'inst', hop) for hop in hops] for p in packed]]
    ppermute x1, waiting for transfers between devices: 0.01 us -> 2.11 us  [section(): lax.ppermute(held, 'inst', swap)]
    pallas_call x5, Pallas kernels: 7.63 us -> 6.49 us  [the longest x3 4.5 us: finish(): pl.pallas_call(functools.partial(finish_kernel, [(w, p, len(got)) for w,...]
    ppermute x2, starting transfers between devices: 2.16 us -> 3.11 us  [section(): got_sums[g].append(lax.ppermute(part, 'inst', hop))]
  transfers between devices with their start and end apart: 7 -> 7, of which waited for: 1 -> 2; matrix products, arithmetic and copies ran while one was open for 0% -> 0% of each run, Pallas kernels for 45% -> 50%
where the time goes in v3:
time: 43.9 us; the launch traced here: 43.7 us
  Pallas kernels  22.6 us (51%)
  waiting for transfers between devices  10.4 us (24%)
  starting transfers between devices  9.86 us (22%)
  between operations  0.8 us (2%)
    pallas_call x1, Pallas kernels, cut_terms(): pl.pallas_call(cut_kernel, in_specs=[IN_VMEM] * 4 + [IN_SMEM], out_specs=...  10.4 us
    ppermute x1, waiting for transfers between devices, section(): got_state = [[lax.ppermute(p, 'inst', hop) for hop in hops] for p in packed]  8.27 us
    ppermute x1, starting transfers between devices, section(): second = lax.ppermute(second, 'brick', odds + [(b, a) for a, b in odds])  4.6 us
    pallas_call x3, Pallas kernels, finish(): pl.pallas_call(functools.partial(finish_kernel, [(w, p, len(got)) for w,...  4.5 us
    pallas_call x1, Pallas kernels, stencil(): pl.pallas_call(functools.partial(stencil_kernel, period), in_specs=[IN_VM...  4.39 us
    ppermute x2, starting transfers between devices, section(): got_sums[g].append(lax.ppermute(part, 'inst', hop))  3.11 us
    ppermute x1, waiting for transfers between devices, section(): lax.ppermute(held, 'inst', swap)  2.11 us
    ppermute x1, starting transfers between devices, section(): got_state = [[lax.ppermute(p, 'inst', hop) for hop in hops] for p in packed]  1.56 us
  transfers between devices with their start and end apart: 7, of which 2 were waited for; matrix products, arithmetic and copies ran while one was open for 0% of the time, Pallas kernels for 50%

profile of v3, /device:TPU:12, one launch (start us, length us, event | category | flops | bytes accessed | tf_op | source)
XLA Modules:
  0.0 43.7 jit_solution(11525299392471426177)
XLA Ops:
  0.6 0.0 copy-start
  0.6 0.1 collective-permute-start
  0.7 1.4 %pack_state.1 = bf16[2,32,4096]{2,1,0:T(8,128)(2,1)S(1)} custom-call(f32[4,5,8,4096]{3,2,1,0:T(8,128)} %state_ref.15), custom_call_target="tpu_custom_call" | custom-call | tf_op jit(solution)/shard_map/pack_state/pallas_call | solution.py:100
  2.2 1.6 %collective-permute-start.5 = (bf16[2,32,4096]{2,1,0:T(8,128)(2,1)S(1)}, bf16[2,32,4096]{2,1,0:T(8,128)(2,1)S(1)}, u32[]{:S(2)}, u32[]{:S(2)}) collective-permute-start(bf16[2,32,4096]{2,1,0:T(8,128)(2,1)S(1)} %pack_state.1), channel_id=1, source_target_pairs={{0,8},{4,12},{8,0},{12,4},{1,9},{5,13},{9,1},{13,5},{2,10},{6,14},... | collective-permute-start | bytes 1572872 | tf_op jit(solution)/shard_map/ppermute | solution.py:451
  3.7 2.1 %collective-permute-done.mate_ref = f32[4,5,8,4096]{3,2,1,0:T(8,128)S(1)} collective-permute-done((f32[4,5,8,4096]{3,2,1,0:T(8,128)}, f32[4,5,8,4096]{3,2,1,0:T(8,128)S(1)}, u32[]{:S(2)}, u32[]{:S(2)}) %collective-permute-start) | collective-permute-done | bytes 2621472 | tf_op jit(solution)/shard_map/ppermute | solution.py:453
  5.8 0.0 copy-done
  5.8 1.3 %send_sums.1 = (bf16[32,10240]{1,0:T(8,128)(2,1)S(1)}, bf16[32,2048]{1,0:T(8,128)(2,1)S(1)}) custom-call(f32[4,5,8,4096]{3,2,1,0:T(8,128)S(1)} %copy-done, f32[4,5,8,4096]{3,2,1,0:T(8,128)S(1)} %collective-permute-done.mate_ref), custom_call_target="tpu_custom_call" | custom-call | tf_op jit(solution)/shard_map/send_sums/pallas_call | solution.py:189
  7.1 0.0 copy-start.1
  7.2 0.0 copy-start.3
  7.2 0.0 copy-start.4
  7.2 0.0 copy-start.5
  7.2 1.6 %collective-permute-start.4 = (bf16[32,10240]{1,0:T(8,128)(2,1)S(1)}, bf16[32,10240]{1,0:T(8,128)(2,1)S(1)}, u32[]{:S(2)}, u32[]{:S(2)}) collective-permute-start(bf16[32,10240]{1,0:T(8,128)(2,1)S(1)} %get-tuple-element.13), channel_id=1, source_target_pairs={{0,8},{4,12},{8,0},{12,4},{1,9},{5,13},{9,1},{13,5},{2,10},{6,14},... | collective-permute-start | bytes 1966088 | tf_op jit(solution)/shard_map/ppermute | solution.py:461
  8.8 8.3 %collective-permute-done.5.refs_0_ = bf16[2,32,4096]{2,1,0:T(8,128)(2,1)S(1)} collective-permute-done((bf16[2,32,4096]{2,1,0:T(8,128)(2,1)S(1)}, bf16[2,32,4096]{2,1,0:T(8,128)(2,1)S(1)}, u32[]{:S(2)}, u32[]{:S(2)}) %collective-permute-start.5) | collective-permute-done | bytes 524320 | tf_op jit(solution)/shard_map/ppermute | solution.py:451
  17.0 0.0 collective-permute-start.6
  17.0 0.6 %pack_edges.1 = (bf16[5,8,4096]{2,1,0:T(8,128)(2,1)S(1)}, bf16[5,8,4096]{2,1,0:T(8,128)(2,1)S(1)}) custom-call(f32[4,5,8,4096]{3,2,1,0:T(8,128)S(1)} %copy-done), custom_call_target="tpu_custom_call" | custom-call | tf_op jit(solution)/shard_map/pack_edges/pallas_call | solution.py:149
  17.6 0.5 %collective-permute-start.1 = (bf16[5,8,4096]{2,1,0:T(8,128)(2,1)S(1)}, bf16[5,8,4096]{2,1,0:T(8,128)(2,1)S(1)}, u32[]{:S(2)}, u32[]{:S(2)}) collective-permute-start(bf16[5,8,4096]{2,1,0:T(8,128)(2,1)S(1)} %get-tuple-element.10), channel_id=1, source_target_pairs={{0,1},{2,3},{1,0},{3,2},{4,5},{6,7},{5,4},{7,6},{8,9},{10,11},{9,8... | collective-permute-start | bytes 983048 | tf_op jit(solution)/shard_map/ppermute | solution.py:456
  18.1 4.6 %collective-permute-start.2 = (bf16[5,8,4096]{2,1,0:T(8,128)(2,1)S(1)}, bf16[5,8,4096]{2,1,0:T(8,128)(2,1)S(1)}, u32[]{:S(2)}, u32[]{:S(2)}) collective-permute-start(bf16[5,8,4096]{2,1,0:T(8,128)(2,1)S(1)} %get-tuple-element.11), channel_id=1, source_target_pairs={{1,2},{2,1},{5,6},{6,5},{9,10},{10,9},{13,14},{14,13},{17,18},{18,... | collective-permute-start | bytes 983048 | tf_op jit(solution)/shard_map/ppermute | solution.py:457
  22.7 1.6 %collective-permute-start.3 = (bf16[32,2048]{1,0:T(8,128)(2,1)S(1)}, bf16[32,2048]{1,0:T(8,128)(2,1)S(1)}, u32[]{:S(2)}, u32[]{:S(2)}) collective-permute-start(bf16[32,2048]{1,0:T(8,128)(2,1)S(1)} %get-tuple-element.12), channel_id=1, source_target_pairs={{0,8},{4,12},{8,0},{12,4},{1,9},{5,13},{9,1},{13,5},{2,10},{6,14},... | collective-permute-start | bytes 393224 | tf_op jit(solution)/shard_map/ppermute | solution.py:461
  24.3 0.0 copy-done.1
  24.3 0.0 copy-done.3
  24.3 0.0 copy-done.4
  24.3 0.0 copy-done.5
  24.3 10.4 %cut_terms.1.cut_ref = f32[4,5,8,4096]{3,2,1,0:T(8,128)S(1)} custom-call(f32[4,5,8,4096]{3,2,1,0:T(8,128)S(1)} %copy-done, bf16[8,320,320]{2,1,0:T(8,128)(2,1)S(1)} %copy-done.1, s32[1,256]{1,0:T(1,128)S(1)} %copy-done.3, s32[1,256]{1,0:T(1,128)S(1)} %copy-done.4, s32[4]{0:T(128)S(1)} %copy-done.5), custom_call_target="tpu_custom_call" | custom-call | tf_op jit(solution)/shard_map/cut_terms/pallas_call | solution.py:295
  34.7 0.0 copy-start.2
  34.7 0.0 collective-permute-done.1.first_ref
  34.8 0.0 collective-permute-done.2.second_ref
  34.8 4.4 %stencil.1.part_ref = f32[4,5,8,4096]{3,2,1,0:T(8,128)S(1)} custom-call(f32[4,5,8,4096]{3,2,1,0:T(8,128)S(1)} %copy-done, f32[4,5,8,4096]{3,2,1,0:T(8,128)S(1)} %collective-permute-done.mate_ref, f32[4,5,8,4096]{3,2,1,0:T(8,128)S(1)} %cut_terms.1.cut_ref, bf16[5,8,4096]{2,1,0:T(8,128)(2,1)S(1)} %collective-permute-done.1.first_ref, ...), custom_call_target="tpu_custom_call" | custom-call | tf_op jit(solution)/shard_map/stencil/pallas_call | solution.py:355
  39.2 0.0 collective-permute-done.6.refs_1_
  39.2 0.0 copy-done.2
  39.2 1.9 %finish.3 = (f32[4,5,8,4096]{3,2,1,0:T(8,128)}, f32[4,5,8,4096]{3,2,1,0:T(8,128)}) custom-call(f32[4,5,8,4096]{3,2,1,0:T(8,128)S(1)} %stencil.1.part_ref, f32[4,5,8,4096]{3,2,1,0:T(8,128)S(1)} %copy-done, f32[8,4096]{1,0:T(8,128)S(1)} %copy-done.2, bf16[2,32,4096]{2,1,0:T(8,128)(2,1)S(1)} %collective-permute-done.5.refs_0_, ...), custom_call_target="tpu_custom_call" | custom-call | tf_op jit(solution)/shard_map/finish/pallas_call | solution.py:424
  41.1 0.0 collective-permute-done.4.refs_0_
  41.1 1.7 %finish.4 = (f32[4,5,8,4096]{3,2,1,0:T(8,128)}, f32[4,5,8,4096]{3,2,1,0:T(8,128)}) custom-call(f32[4,5,8,4096]{3,2,1,0:T(8,128)S(1)} %stencil.1.part_ref, f32[4,5,8,4096]{3,2,1,0:T(8,128)S(1)} %copy-done, f32[8,4096]{1,0:T(8,128)S(1)} %copy-done.2, ...), custom_call_target="tpu_custom_call", output_to_operand_aliasing={{0}: (4, {}), {1}: (5, {})} | custom-call | tf_op jit(solution)/shard_map/finish/pallas_call | solution.py:424
  42.8 0.0 collective-permute-done.3.refs_0_
  42.8 0.9 %finish.5 = (f32[4,5,8,4096]{3,2,1,0:T(8,128)}, f32[4,5,8,4096]{3,2,1,0:T(8,128)}) custom-call(f32[4,5,8,4096]{3,2,1,0:T(8,128)S(1)} %stencil.1.part_ref, f32[4,5,8,4096]{3,2,1,0:T(8,128)S(1)} %copy-done, f32[8,4096]{1,0:T(8,128)S(1)} %copy-done.2, ...), custom_call_target="tpu_custom_call", output_to_operand_aliasing={{0}: (4, {}), {1}: (5, {})} | custom-call | tf_op jit(solution)/shard_map/finish/pallas_call | solution.py:424
Async XLA Ops:
  0.6 5.2 %copy-start = (f32[4,5,8,4096]{3,2,1,0:T(8,128)S(1)}, f32[4,5,8,4096]{3,2,1,0:T(8,128)}, u32[]{:S(2)}) copy-start(f32[4,5,8,4096]{3,2,1,0:T(8,128)} %state_ref.15) | copy-start | bytes 7864324
  0.6 5.2 %collective-permute-start = (f32[4,5,8,4096]{3,2,1,0:T(8,128)}, f32[4,5,8,4096]{3,2,1,0:T(8,128)S(1)}, u32[]{:S(2)}, u32[]{:S(2)}) collective-permute-start(f32[4,5,8,4096]{3,2,1,0:T(8,128)} %state_ref.15), channel_id=1, source_target_pairs={{0,4},{4,0},{8,12},{12,8},{1,5},{5,1},{9,13},{13,9},{2,6},{6,2},{1... | collective-permute-start | bytes 7864328 | tf_op jit(solution)/shard_map/ppermute | solution.py:453
  2.2 14.9 %collective-permute-start.5 = (bf16[2,32,4096]{2,1,0:T(8,128)(2,1)S(1)}, bf16[2,32,4096]{2,1,0:T(8,128)(2,1)S(1)}, u32[]{:S(2)}, u32[]{:S(2)}) collective-permute-start(bf16[2,32,4096]{2,1,0:T(8,128)(2,1)S(1)} %pack_state.1), channel_id=1, source_target_pairs={{0,8},{4,12},{8,0},{12,4},{1,9},{5,13},{9,1},{13,5},{2,10},{6,14},... | collective-permute-start | bytes 1572872 | tf_op jit(solution)/shard_map/ppermute | solution.py:451
  7.1 17.1 %copy-start.1 = (bf16[8,320,320]{2,1,0:T(8,128)(2,1)S(1)}, bf16[8,320,320]{2,1,0:T(8,128)(2,1)}, u32[]{:S(2)}) copy-start(bf16[8,320,320]{2,1,0:T(8,128)(2,1)} %blocks_ref.1) | copy-start | bytes 4915204
  7.2 17.1 %copy-start.3 = (s32[1,256]{1,0:T(1,128)S(1)}, s32[1,256]{1,0:T(1,128)}, u32[]{:S(2)}) copy-start(s32[1,256]{1,0:T(1,128)} %index_ref.1) | copy-start | bytes 3076
  7.2 17.1 %copy-start.4 = (s32[1,256]{1,0:T(1,128)S(1)}, s32[1,256]{1,0:T(1,128)}, u32[]{:S(2)}) copy-start(s32[1,256]{1,0:T(1,128)} %type_ref.1) | copy-start | bytes 3076
  7.2 17.1 %copy-start.5 = (s32[4]{0:T(128)S(1)}, s32[4]{0:T(128)}, u32[]{:S(2)}) copy-start(s32[4]{0:T(128)} %count_ref.1) | copy-start | bytes 52
  7.2 33.9 %collective-permute-start.4 = (bf16[32,10240]{1,0:T(8,128)(2,1)S(1)}, bf16[32,10240]{1,0:T(8,128)(2,1)S(1)}, u32[]{:S(2)}, u32[]{:S(2)}) collective-permute-start(bf16[32,10240]{1,0:T(8,128)(2,1)S(1)} %get-tuple-element.13), channel_id=1, source_target_pairs={{0,8},{4,12},{8,0},{12,4},{1,9},{5,13},{9,1},{13,5},{2,10},{6,14},... | collective-permute-start | bytes 1966088 | tf_op jit(solution)/shard_map/ppermute | solution.py:461
  17.0 22.1 %collective-permute-start.6 = (bf16[2,32,4096]{2,1,0:T(8,128)(2,1)S(1)}, bf16[2,32,4096]{2,1,0:T(8,128)(2,1)S(1)}, u32[]{:S(2)}, u32[]{:S(2)}) collective-permute-start(bf16[2,32,4096]{2,1,0:T(8,128)(2,1)S(1)} %collective-permute-done.5.refs_0_), channel_id=1, source_target_pairs={{0,4},{4,0},{8,12},{12,8},{1,5},{5,1},{9,13},{13,9},{2,6},{6,2},{1... | collective-permute-start | bytes 1572872 | tf_op jit(solution)/shard_map/ppermute | solution.py:468
  17.6 17.2 %collective-permute-start.1 = (bf16[5,8,4096]{2,1,0:T(8,128)(2,1)S(1)}, bf16[5,8,4096]{2,1,0:T(8,128)(2,1)S(1)}, u32[]{:S(2)}, u32[]{:S(2)}) collective-permute-start(bf16[5,8,4096]{2,1,0:T(8,128)(2,1)S(1)} %get-tuple-element.10), channel_id=1, source_target_pairs={{0,1},{2,3},{1,0},{3,2},{4,5},{6,7},{5,4},{7,6},{8,9},{10,11},{9,8... | collective-permute-start | bytes 983048 | tf_op jit(solution)/shard_map/ppermute | solution.py:456
  18.1 16.7 %collective-permute-start.2 = (bf16[5,8,4096]{2,1,0:T(8,128)(2,1)S(1)}, bf16[5,8,4096]{2,1,0:T(8,128)(2,1)S(1)}, u32[]{:S(2)}, u32[]{:S(2)}) collective-permute-start(bf16[5,8,4096]{2,1,0:T(8,128)(2,1)S(1)} %get-tuple-element.11), channel_id=1, source_target_pairs={{1,2},{2,1},{5,6},{6,5},{9,10},{10,9},{13,14},{14,13},{17,18},{18,... | collective-permute-start | bytes 983048 | tf_op jit(solution)/shard_map/ppermute | solution.py:457
  22.7 20.1 %collective-permute-start.3 = (bf16[32,2048]{1,0:T(8,128)(2,1)S(1)}, bf16[32,2048]{1,0:T(8,128)(2,1)S(1)}, u32[]{:S(2)}, u32[]{:S(2)}) collective-permute-start(bf16[32,2048]{1,0:T(8,128)(2,1)S(1)} %get-tuple-element.12), channel_id=1, source_target_pairs={{0,8},{4,12},{8,0},{12,4},{1,9},{5,13},{9,1},{13,5},{2,10},{6,14},... | collective-permute-start | bytes 393224 | tf_op jit(solution)/shard_map/ppermute | solution.py:461
  34.7 4.4 %copy-start.2 = (f32[8,4096]{1,0:T(8,128)S(1)}, f32[8,4096]{1,0:T(8,128)}, u32[]{:S(2)}) copy-start(f32[8,4096]{1,0:T(8,128)} %step_ref.5) | copy-start | bytes 393220

commit v4 on v3

--- a/solution.py
+++ b/solution.py
@@ -125,33 +125,44 @@
     )(state)
 
 
-def pack_edges_kernel(state_ref, first_ref, second_ref):
+def pack_edges_kernel(state_ref, held_ref, first_ref, second_ref, sems):
     inst, nvar, rows, cells = state_ref.shape
+    chunks = sems.shape[0]
+    width = cells // chunks
     odd = lax.axis_index("brick") % 2 == 1
+    copies = []
+    for c in range(chunks):
+        cols = pl.ds(c * width, width)
+        copies.append(pltpu.make_async_copy(state_ref.at[:, :, :, cols], held_ref.at[:, :, :, cols], sems.at[c]))
+        copies[-1].start()
     pair = lax.broadcasted_iota(jnp.int32, (rows, LANES), 0) // 2
-
-    def body(cols, _):
-        for v in range(nvar):
-            q = [state_ref[j, v, :, cols] for j in range(inst)]
-            head, tail = q[0], turn(q[0], 2)
-            for j in range(1, inst):
-                head = jnp.where(pair == j, turn(q[j], 2 * j), head)
-                tail = jnp.where(pair == j, turn(q[j], 2 * j + 2), tail)
-            first_ref[v, :, cols] = jnp.where(odd, head, tail).astype(jnp.bfloat16)
-            second_ref[v, :, cols] = jnp.where(odd, tail, head).astype(jnp.bfloat16)
-
-    columns(cells, LANES, body)
-
-
-def pack_edges(state):
+    for c in range(chunks):
+        copies[c].wait()
+
+        def body(cols, _, base=c * width):
+            at = pl.ds(pl.multiple_of(base + cols.start, LANES), LANES)
+            for v in range(nvar):
+                q = [held_ref[j, v, :, at] for j in range(inst)]
+                head, tail = q[0], pltpu.roll(q[0], 2, 0)
+                for j in range(1, inst):
+                    head = jnp.where(pair == j, pltpu.roll(q[j], 2 * j, 0), head)
+                    tail = jnp.where(pair == j, pltpu.roll(q[j], (2 * j + 2) % rows, 0) if (2 * j + 2) % rows else q[j], tail)
+                first_ref[v, :, at] = jnp.where(odd, head, tail).astype(jnp.bfloat16)
+                second_ref[v, :, at] = jnp.where(odd, tail, head).astype(jnp.bfloat16)
+
+        columns(width, LANES, body)
+
+
+def pack_edges(state, chunks=4):
     _, nvar, rows, cells = state.shape
     edge = pltpu.VMEM((nvar, rows, cells), jnp.bfloat16)
     return pl.pallas_call(
         pack_edges_kernel,
-        in_specs=[IN_VMEM],
-        out_specs=[IN_VMEM] * 2,
-        out_shape=[edge, edge],
-        compiler_params=params(2),
+        in_specs=[IN_HBM],
+        out_specs=[IN_VMEM] * 3,
+        out_shape=[pltpu.VMEM(state.shape, jnp.float32), edge, edge],
+        scratch_shapes=[pltpu.SemaphoreType.DMA((chunks,))],
+        compiler_params=params(4),
         name="pack_edges",
     )(state)
 
@@ -320,13 +331,12 @@
     parity = lax.axis_index("inst") % 2
     odd = lax.axis_index("brick") % 2 == 1
     coefs = [row_coefs(j, inst, period, 0, parity) for j in range(inst)]
+    shares = [sum(c) for c in coefs]
     row = lax.broadcasted_iota(jnp.int32, (rows, LANES), 0)
 
     def body(cols, _):
-        times, above, below = [], [], []
+        above, below = [], []
         for v in range(nvar):
-            values = [centred(ref[k, v, :, cols], v) for ref in (state_ref, mate_ref) for k in range(inst)]
-            times.append([weighted(coefs[j], values) for j in range(inst)])
             first = first_ref[v, :, cols].astype(jnp.float32)
             second = second_ref[v, :, cols].astype(jnp.float32)
             above.append(jnp.where(odd, second, first))
@@ -345,7 +355,11 @@
                 smooth.append(EPS_FOURTH * ((two + back2) - 4.0 * (one + back) + 6.0 * x))
             fup, fdown = flux_of(up), flux_of(down)
             for v in range(nvar):
-                total = 0.5 * (fup[v] - fdown[v]) + smooth[v] + times[v][j]
+                values = [ref[k, v, :, cols] for ref in (state_ref, mate_ref) for k in range(inst)]
+                times = weighted(coefs[j], values)
+                if CENTRE[v]:
+                    times = times - CENTRE[v] * shares[j]
+                total = 0.5 * (fup[v] - fdown[v]) + smooth[v] + times
                 out_ref[j, v, :, cols] = total + cut_ref[j, v, :, cols]
 
     columns(cells, LANES, body)
@@ -445,11 +459,11 @@
     swap = [(i, i ^ 1) for i in range(groups)]
     hops = [[(i, (i + 2 * q) % groups) for i in range(groups)] for q in range(1, groups // 2)]
     cells = state.shape[3]
-    packed = [pack_state(pltpu.with_memory_space_constraint(state, pltpu.HBM), STATE_GROUPS[0])]
-    held = pltpu.with_memory_space_constraint(state, pltpu.VMEM)
+    state = pltpu.with_memory_space_constraint(state, pltpu.HBM)
+    packed = [pack_state(state, STATE_GROUPS[0])]
+    held, first, second = pack_edges(state)
     packed += [pack_more(held, group) for group in STATE_GROUPS[1:]]
     got_state = [[lax.ppermute(p, "inst", hop) for hop in hops] for p in packed]
-    first, second = pack_edges(held)
     mate = pltpu.with_memory_space_constraint(lax.ppermute(held, "inst", swap), pltpu.VMEM)
     evens = [(b, b + 1) for b in range(0, bricks - 1, 2)]
     odds = [(b, b + 1) for b in range(1, bricks - 1, 2)]

time: 43.9 us -> 44.8 us (1.021)
  Pallas kernels: 22.6 us -> 23.6 us
    pallas_call x1, Pallas kernels: 0.56 us -> 1.85 us  [pack_edges(): pl.pallas_call(pack_edges_kernel, in_specs=[IN_HBM], out_specs=[IN_VMEM]...]
  transfers between devices with their start and end apart: 7 -> 7, of which waited for: 2 -> 2; matrix products, arithmetic and copies ran while one was open for 0% -> 0% of each run, Pallas kernels for 50% -> 47%
where the time goes in v4:
time: 44.8 us; the launch traced here: 44.6 us
  Pallas kernels  23.6 us (53%)
  waiting for transfers between devices  10.4 us (23%)
  starting transfers between devices  9.79 us (22%)
  between operations  0.79 us (2%)
    pallas_call x1, Pallas kernels, cut_terms(): pl.pallas_call(cut_kernel, in_specs=[IN_VMEM] * 4 + [IN_SMEM], out_specs=...  10.4 us
    ppermute x1, waiting for transfers between devices, section(): got_state = [[lax.ppermute(p, 'inst', hop) for hop in hops] for p in packed]  8.44 us
    ppermute x1, starting transfers between devices, section(): second = lax.ppermute(second, 'brick', odds + [(b, a) for a, b in odds])  4.6 us
    pallas_call x3, Pallas kernels, finish(): pl.pallas_call(functools.partial(finish_kernel, [(w, p, len(got)) for w,...  4.5 us
    pallas_call x1, Pallas kernels, stencil(): pl.pallas_call(functools.partial(stencil_kernel, period), in_specs=[IN_VM...  4.2 us
    ppermute x2, starting transfers between devices, section(): got_sums[g].append(lax.ppermute(part, 'inst', hop))  3.11 us
    ppermute x1, waiting for transfers between devices, section(): lax.ppermute(held, 'inst', swap)  1.99 us
    pallas_call x1, Pallas kernels, pack_edges(): pl.pallas_call(pack_edges_kernel, in_specs=[IN_HBM], out_specs=[IN_VMEM]...  1.85 us
  transfers between devices with their start and end apart: 7, of which 2 were waited for; matrix products, arithmetic and copies ran while one was open for 0% of the time, Pallas kernels for 47%

profile of v4, /device:TPU:12, one launch (start us, length us, event | category | flops | bytes accessed | tf_op | source)
XLA Modules:
  0.0 44.6 jit_solution(17270042956112915536)
XLA Ops:
  0.6 1.9 %pack_edges.1 = (f32[4,5,8,4096]{3,2,1,0:T(8,128)S(1)}, bf16[5,8,4096]{2,1,0:T(8,128)(2,1)S(1)}, bf16[5,8,4096]{2,1,0:T(8,128)(2,1)S(1)}) custom-call(f32[4,5,8,4096]{3,2,1,0:T(8,128)} %state_ref.3), custom_call_target="tpu_custom_call" | custom-call | tf_op jit(solution)/shard_map/pack_edges/pallas_call | solution.py:159
  2.5 0.1 collective-permute-start
  2.6 1.3 %pack_state.1 = bf16[2,32,4096]{2,1,0:T(8,128)(2,1)S(1)} custom-call(f32[4,5,8,4096]{3,2,1,0:T(8,128)} %state_ref.3), custom_call_target="tpu_custom_call" | custom-call | tf_op jit(solution)/shard_map/pack_state/pallas_call | solution.py:100
  3.9 0.0 copy-start
  3.9 0.0 copy-start.2
  3.9 0.0 copy-start.3
  3.9 0.0 copy-start.4
  3.9 1.6 %collective-permute-start.5 = (bf16[2,32,4096]{2,1,0:T(8,128)(2,1)S(1)}, bf16[2,32,4096]{2,1,0:T(8,128)(2,1)S(1)}, u32[]{:S(2)}, u32[]{:S(2)}) collective-permute-start(bf16[2,32,4096]{2,1,0:T(8,128)(2,1)S(1)} %pack_state.1), channel_id=1, source_target_pairs={{0,8},{4,12},{8,0},{12,4},{1,9},{5,13},{9,1},{13,5},{2,10},{6,14},... | collective-permute-start | bytes 1572872 | tf_op jit(solution)/shard_map/ppermute | solution.py:466
  5.5 2.0 %collective-permute-done.mate_ref = f32[4,5,8,4096]{3,2,1,0:T(8,128)S(1)} collective-permute-done((f32[4,5,8,4096]{3,2,1,0:T(8,128)S(1)}, f32[4,5,8,4096]{3,2,1,0:T(8,128)S(1)}, u32[]{:S(2)}, u32[]{:S(2)}) %collective-permute-start) | collective-permute-done | bytes 2621472 | tf_op jit(solution)/shard_map/ppermute | solution.py:467
  7.5 1.3 %send_sums.1 = (bf16[32,10240]{1,0:T(8,128)(2,1)S(1)}, bf16[32,2048]{1,0:T(8,128)(2,1)S(1)}) custom-call(f32[4,5,8,4096]{3,2,1,0:T(8,128)S(1)} %get-tuple-element.11.state_ref, f32[4,5,8,4096]{3,2,1,0:T(8,128)S(1)} %collective-permute-done.mate_ref), custom_call_target="tpu_custom_call" | custom-call | tf_op jit(solution)/shard_map/send_sums/pallas_call | solution.py:200
  8.8 1.6 %collective-permute-start.4 = (bf16[32,10240]{1,0:T(8,128)(2,1)S(1)}, bf16[32,10240]{1,0:T(8,128)(2,1)S(1)}, u32[]{:S(2)}, u32[]{:S(2)}) collective-permute-start(bf16[32,10240]{1,0:T(8,128)(2,1)S(1)} %get-tuple-element.15), channel_id=1, source_target_pairs={{0,8},{4,12},{8,0},{12,4},{1,9},{5,13},{9,1},{13,5},{2,10},{6,14},... | collective-permute-start | bytes 1966088 | tf_op jit(solution)/shard_map/ppermute | solution.py:475
  10.3 8.4 %collective-permute-done.5.refs_0_ = bf16[2,32,4096]{2,1,0:T(8,128)(2,1)S(1)} collective-permute-done((bf16[2,32,4096]{2,1,0:T(8,128)(2,1)S(1)}, bf16[2,32,4096]{2,1,0:T(8,128)(2,1)S(1)}, u32[]{:S(2)}, u32[]{:S(2)}) %collective-permute-start.5) | collective-permute-done | bytes 524320 | tf_op jit(solution)/shard_map/ppermute | solution.py:466
  18.8 0.0 collective-permute-start.6
  18.8 0.5 %collective-permute-start.1 = (bf16[5,8,4096]{2,1,0:T(8,128)(2,1)S(1)}, bf16[5,8,4096]{2,1,0:T(8,128)(2,1)S(1)}, u32[]{:S(2)}, u32[]{:S(2)}) collective-permute-start(bf16[5,8,4096]{2,1,0:T(8,128)(2,1)S(1)} %get-tuple-element.12), channel_id=1, source_target_pairs={{0,1},{2,3},{1,0},{3,2},{4,5},{6,7},{5,4},{7,6},{8,9},{10,11},{9,8... | collective-permute-start | bytes 983048 | tf_op jit(solution)/shard_map/ppermute | solution.py:470
  19.2 4.6 %collective-permute-start.2 = (bf16[5,8,4096]{2,1,0:T(8,128)(2,1)S(1)}, bf16[5,8,4096]{2,1,0:T(8,128)(2,1)S(1)}, u32[]{:S(2)}, u32[]{:S(2)}) collective-permute-start(bf16[5,8,4096]{2,1,0:T(8,128)(2,1)S(1)} %get-tuple-element.13), channel_id=1, source_target_pairs={{1,2},{2,1},{5,6},{6,5},{9,10},{10,9},{13,14},{14,13},{17,18},{18,... | collective-permute-start | bytes 983048 | tf_op jit(solution)/shard_map/ppermute | solution.py:471
  23.8 1.6 %collective-permute-start.3 = (bf16[32,2048]{1,0:T(8,128)(2,1)S(1)}, bf16[32,2048]{1,0:T(8,128)(2,1)S(1)}, u32[]{:S(2)}, u32[]{:S(2)}) collective-permute-start(bf16[32,2048]{1,0:T(8,128)(2,1)S(1)} %get-tuple-element.14), channel_id=1, source_target_pairs={{0,8},{4,12},{8,0},{12,4},{1,9},{5,13},{9,1},{13,5},{2,10},{6,14},... | collective-permute-start | bytes 393224 | tf_op jit(solution)/shard_map/ppermute | solution.py:475
  25.4 0.0 copy-done
  25.4 0.0 copy-done.2
  25.4 0.0 copy-done.3
  25.4 0.0 copy-done.4
  25.4 10.4 %cut_terms.1.cut_ref = f32[4,5,8,4096]{3,2,1,0:T(8,128)S(1)} custom-call(f32[4,5,8,4096]{3,2,1,0:T(8,128)S(1)} %get-tuple-element.11.state_ref, bf16[8,320,320]{2,1,0:T(8,128)(2,1)S(1)} %copy-done, s32[1,256]{1,0:T(1,128)S(1)} %copy-done.2, s32[1,256]{1,0:T(1,128)S(1)} %copy-done.3, s32[4]{0:T(128)S(1)} %copy-done.4), custom_call_target="tpu_custom_call" | custom-call | tf_op jit(solution)/shard_map/cut_terms/pallas_call | solution.py:306
  35.9 0.0 copy-start.1
  35.9 0.0 collective-permute-done.1.first_ref
  35.9 0.0 collective-permute-done.2.second_ref
  35.9 4.2 %stencil.1.part_ref = f32[4,5,8,4096]{3,2,1,0:T(8,128)S(1)} custom-call(f32[4,5,8,4096]{3,2,1,0:T(8,128)S(1)} %get-tuple-element.11.state_ref, f32[4,5,8,4096]{3,2,1,0:T(8,128)S(1)} %collective-permute-done.mate_ref, f32[4,5,8,4096]{3,2,1,0:T(8,128)S(1)} %cut_terms.1.cut_ref, bf16[5,8,4096]{2,1,0:T(8,128)(2,1)S(1)} %collective-permute-done.1.first_ref, ...), custom_call_target="tpu_custom_call" | custom-call | tf_op jit(solution)/shard_map/stencil/pallas_call | solution.py:369
  40.1 0.0 collective-permute-done.6.refs_1_
  40.1 0.0 copy-done.1
  40.1 1.9 %finish.3 = (f32[4,5,8,4096]{3,2,1,0:T(8,128)}, f32[4,5,8,4096]{3,2,1,0:T(8,128)}) custom-call(f32[4,5,8,4096]{3,2,1,0:T(8,128)S(1)} %stencil.1.part_ref, f32[4,5,8,4096]{3,2,1,0:T(8,128)S(1)} %get-tuple-element.11.state_ref, f32[8,4096]{1,0:T(8,128)S(1)} %copy-done.1, bf16[2,32,4096]{2,1,0:T(8,128)(2,1)S(1)} %collective-permute-done.5.refs_0_, ...), custom_call_target="tpu_custom_call" | custom-call | tf_op jit(solution)/shard_map/finish/pallas_call | solution.py:438
  42.0 0.0 collective-permute-done.4.refs_0_
  42.0 1.7 %finish.4 = (f32[4,5,8,4096]{3,2,1,0:T(8,128)}, f32[4,5,8,4096]{3,2,1,0:T(8,128)}) custom-call(f32[4,5,8,4096]{3,2,1,0:T(8,128)S(1)} %stencil.1.part_ref, f32[4,5,8,4096]{3,2,1,0:T(8,128)S(1)} %get-tuple-element.11.state_ref, f32[8,4096]{1,0:T(8,128)S(1)} %copy-done.1, ...), custom_call_target="tpu_custom_call", output_to_operand_aliasing={{0}: (4, {}), {1}: (5, {})} | custom-call | tf_op jit(solution)/shard_map/finish/pallas_call | solution.py:438
  43.7 0.0 collective-permute-done.3.refs_0_
  43.8 0.9 %finish.5 = (f32[4,5,8,4096]{3,2,1,0:T(8,128)}, f32[4,5,8,4096]{3,2,1,0:T(8,128)}) custom-call(f32[4,5,8,4096]{3,2,1,0:T(8,128)S(1)} %stencil.1.part_ref, f32[4,5,8,4096]{3,2,1,0:T(8,128)S(1)} %get-tuple-element.11.state_ref, f32[8,4096]{1,0:T(8,128)S(1)} %copy-done.1, ...), custom_call_target="tpu_custom_call", output_to_operand_aliasing={{0}: (4, {}), {1}: (5, {})} | custom-call | tf_op jit(solution)/shard_map/finish/pallas_call | solution.py:438
Async XLA Ops:
  2.5 5.0 %collective-permute-start = (f32[4,5,8,4096]{3,2,1,0:T(8,128)S(1)}, f32[4,5,8,4096]{3,2,1,0:T(8,128)S(1)}, u32[]{:S(2)}, u32[]{:S(2)}) collective-permute-start(f32[4,5,8,4096]{3,2,1,0:T(8,128)S(1)} %get-tuple-element.11.state_ref), channel_id=1, source_target_pairs={{0,4},{4,0},{8,12},{12,8},{1,5},{5,1},{9,13},{13,9},{2,6},{6,2},{1... | collective-permute-start | bytes 7864328 | tf_op jit(solution)/shard_map/ppermute | solution.py:467
  3.9 21.5 %copy-start = (bf16[8,320,320]{2,1,0:T(8,128)(2,1)S(1)}, bf16[8,320,320]{2,1,0:T(8,128)(2,1)}, u32[]{:S(2)}) copy-start(bf16[8,320,320]{2,1,0:T(8,128)(2,1)} %blocks_ref.1) | copy-start | bytes 4915204
  3.9 21.5 %copy-start.2 = (s32[1,256]{1,0:T(1,128)S(1)}, s32[1,256]{1,0:T(1,128)}, u32[]{:S(2)}) copy-start(s32[1,256]{1,0:T(1,128)} %index_ref.1) | copy-start | bytes 3076
  3.9 21.5 %copy-start.3 = (s32[1,256]{1,0:T(1,128)S(1)}, s32[1,256]{1,0:T(1,128)}, u32[]{:S(2)}) copy-start(s32[1,256]{1,0:T(1,128)} %type_ref.1) | copy-start | bytes 3076
  3.9 21.5 %copy-start.4 = (s32[4]{0:T(128)S(1)}, s32[4]{0:T(128)}, u32[]{:S(2)}) copy-start(s32[4]{0:T(128)} %count_ref.1) | copy-start | bytes 52
  3.9 14.9 %collective-permute-start.5 = (bf16[2,32,4096]{2,1,0:T(8,128)(2,1)S(1)}, bf16[2,32,4096]{2,1,0:T(8,128)(2,1)S(1)}, u32[]{:S(2)}, u32[]{:S(2)}) collective-permute-start(bf16[2,32,4096]{2,1,0:T(8,128)(2,1)S(1)} %pack_state.1), channel_id=1, source_target_pairs={{0,8},{4,12},{8,0},{12,4},{1,9},{5,13},{9,1},{13,5},{2,10},{6,14},... | collective-permute-start | bytes 1572872 | tf_op jit(solution)/shard_map/ppermute | solution.py:466
  8.8 33.2 %collective-permute-start.4 = (bf16[32,10240]{1,0:T(8,128)(2,1)S(1)}, bf16[32,10240]{1,0:T(8,128)(2,1)S(1)}, u32[]{:S(2)}, u32[]{:S(2)}) collective-permute-start(bf16[32,10240]{1,0:T(8,128)(2,1)S(1)} %get-tuple-element.15), channel_id=1, source_target_pairs={{0,8},{4,12},{8,0},{12,4},{1,9},{5,13},{9,1},{13,5},{2,10},{6,14},... | collective-permute-start | bytes 1966088 | tf_op jit(solution)/shard_map/ppermute | solution.py:475
  18.8 21.3 %collective-permute-start.6 = (bf16[2,32,4096]{2,1,0:T(8,128)(2,1)S(1)}, bf16[2,32,4096]{2,1,0:T(8,128)(2,1)S(1)}, u32[]{:S(2)}, u32[]{:S(2)}) collective-permute-start(bf16[2,32,4096]{2,1,0:T(8,128)(2,1)S(1)} %collective-permute-done.5.refs_0_), channel_id=1, source_target_pairs={{0,4},{4,0},{8,12},{12,8},{1,5},{5,1},{9,13},{13,9},{2,6},{6,2},{1... | collective-permute-start | bytes 1572872 | tf_op jit(solution)/shard_map/ppermute | solution.py:482
  18.8 17.1 %collective-permute-start.1 = (bf16[5,8,4096]{2,1,0:T(8,128)(2,1)S(1)}, bf16[5,8,4096]{2,1,0:T(8,128)(2,1)S(1)}, u32[]{:S(2)}, u32[]{:S(2)}) collective-permute-start(bf16[5,8,4096]{2,1,0:T(8,128)(2,1)S(1)} %get-tuple-element.12), channel_id=1, source_target_pairs={{0,1},{2,3},{1,0},{3,2},{4,5},{6,7},{5,4},{7,6},{8,9},{10,11},{9,8... | collective-permute-start | bytes 983048 | tf_op jit(solution)/shard_map/ppermute | solution.py:470
  19.2 16.6 %collective-permute-start.2 = (bf16[5,8,4096]{2,1,0:T(8,128)(2,1)S(1)}, bf16[5,8,4096]{2,1,0:T(8,128)(2,1)S(1)}, u32[]{:S(2)}, u32[]{:S(2)}) collective-permute-start(bf16[5,8,4096]{2,1,0:T(8,128)(2,1)S(1)} %get-tuple-element.13), channel_id=1, source_target_pairs={{1,2},{2,1},{5,6},{6,5},{9,10},{10,9},{13,14},{14,13},{17,18},{18,... | collective-permute-start | bytes 983048 | tf_op jit(solution)/shard_map/ppermute | solution.py:471
  23.8 19.9 %collective-permute-start.3 = (bf16[32,2048]{1,0:T(8,128)(2,1)S(1)}, bf16[32,2048]{1,0:T(8,128)(2,1)S(1)}, u32[]{:S(2)}, u32[]{:S(2)}) collective-permute-start(bf16[32,2048]{1,0:T(8,128)(2,1)S(1)} %get-tuple-element.14), channel_id=1, source_target_pairs={{0,8},{4,12},{8,0},{12,4},{1,9},{5,13},{9,1},{13,5},{2,10},{6,14},... | collective-permute-start | bytes 393224 | tf_op jit(solution)/shard_map/ppermute | solution.py:475
  35.9 4.2 %copy-start.1 = (f32[8,4096]{1,0:T(8,128)S(1)}, f32[8,4096]{1,0:T(8,128)}, u32[]{:S(2)}) copy-start(f32[8,4096]{1,0:T(8,128)} %step_ref.5) | copy-start | bytes 393220

commit v5 on v4

--- a/solution.py
+++ b/solution.py
@@ -15,7 +15,7 @@
 UNROLL = 2
 MIB = 1 << 20
 CENTRE = (1.25, 0.0, 0.0, 0.0, 2.75)
-STATE_GROUPS = ((1, 2),)
+STATE_GROUPS = ((1,), (2,))
 PARTS = 2
 SUM_GROUPS = (((3, 0, 2), (4, 0, 2), (0, 0, 1)), ((0, 1, 2),))
 
@@ -94,7 +94,7 @@
         pack_columns(lambda k, n, at: held_ref[k, n, :, at], variables, inst, out_ref, c * width, width)
 
 
-def pack_state(state, variables, chunks=4):
+def pack_state(state, variables, chunks=2):
     inst, _, rows, cells = state.shape
     n = len(variables)
     return pl.pallas_call(
@@ -211,7 +211,7 @@
     return -(-size // LANES) * LANES
 
 
-def cut_kernel(state_ref, blocks_ref, index_ref, type_ref, count_ref, out_ref, tiles_ref, wide_ref, lhs_ref, back_ref):
+def cut_kernel(state_ref, blocks_ref, index_ref, type_ref, count_ref, back_ref, tiles_ref, wide_ref, lhs_ref):
     inst, nvar, rows, cells = state_ref.shape
     kinds, size, _ = blocks_ref.shape
     slots = index_ref.shape[1]
@@ -280,22 +280,6 @@
     give = jnp.concatenate([give, give], axis=1)
     back_ref[...] = jnp.dot(give, tiles_ref[0:2 * slots, :], preferred_element_type=jnp.float32)
 
-    def scatter(cols, c):
-        row = pl.multiple_of(c * rows, rows)
-        first = lax.broadcasted_iota(jnp.int32, (rows, LANES), 1) < TILE
-        for i in range(inst):
-            for v in range(nvar):
-                at = pl.ds(i * wide + v // 2 * LANES, LANES)
-                lo = back_ref[pl.ds(row, rows), at]
-                hi = back_ref[pl.ds(half + row, rows), at]
-                if v % 2 == 0:
-                    hi = pltpu.roll(hi, TILE, 1)
-                else:
-                    lo = pltpu.roll(lo, TILE, 1)
-                out_ref[i, v, :, cols] = jnp.where(first, lo, hi)
-
-    columns(cells, LANES, scatter)
-
 
 def cut_terms(state, blocks, index, types, counts):
     inst, _, rows, cells = state.shape
@@ -307,12 +291,11 @@
         cut_kernel,
         in_specs=[IN_VMEM] * 4 + [IN_SMEM],
         out_specs=IN_VMEM,
-        out_shape=pltpu.VMEM(state.shape, jnp.float32),
+        out_shape=pltpu.VMEM((tiles, inst * wide), jnp.float32),
         scratch_shapes=[
             pltpu.VMEM((max(tiles, 2 * slots), inst * wide), jnp.bfloat16),
             pltpu.VMEM((wide, kinds * wide), jnp.bfloat16),
             pltpu.VMEM((inst * slots, kinds * wide), jnp.bfloat16),
-            pltpu.VMEM((tiles, inst * wide), jnp.float32),
         ],
         compiler_params=params(24),
         name="cut_terms",
@@ -333,9 +316,12 @@
     coefs = [row_coefs(j, inst, period, 0, parity) for j in range(inst)]
     shares = [sum(c) for c in coefs]
     row = lax.broadcasted_iota(jnp.int32, (rows, LANES), 0)
-
-    def body(cols, _):
+    left = lax.broadcasted_iota(jnp.int32, (rows, LANES), 1) < TILE
+    half, wide = cut_ref.shape[0] // 2, cut_ref.shape[1] // inst
+
+    def body(cols, c):
         above, below = [], []
+        at = pl.multiple_of(c * rows, rows)
         for v in range(nvar):
             first = first_ref[v, :, cols].astype(jnp.float32)
             second = second_ref[v, :, cols].astype(jnp.float32)
@@ -360,7 +346,13 @@
                 if CENTRE[v]:
                     times = times - CENTRE[v] * shares[j]
                 total = 0.5 * (fup[v] - fdown[v]) + smooth[v] + times
-                out_ref[j, v, :, cols] = total + cut_ref[j, v, :, cols]
+                lanes = pl.ds(j * wide + v // 2 * LANES, LANES)
+                lo, hi = cut_ref[pl.ds(at, rows), lanes], cut_ref[pl.ds(half + at, rows), lanes]
+                if v % 2 == 0:
+                    hi = pltpu.roll(hi, TILE, 1)
+                else:
+                    lo = pltpu.roll(lo, TILE, 1)
+                out_ref[j, v, :, cols] = total + jnp.where(left, lo, hi)
 
     columns(cells, LANES, body)
 

time: 44.8 us -> 56.6 us (1.26)
  the two profiles are of different devices: /device:TPU:12 before, /device:TPU:0 now
where the time goes in v5:
time: 56.6 us; the launch traced here: 56.4 us
  waiting for transfers between devices  25.1 us (44%)
  Pallas kernels  20.9 us (37%)
  starting transfers between devices  9.62 us (17%)
  between operations  0.79 us (1%)
    ppermute x2, waiting for transfers between devices, section(): got_state = [[lax.ppermute(p, 'inst', hop) for hop in hops] for p in packed]  20.5 us
    pallas_call x1, Pallas kernels, cut_terms(): pl.pallas_call(cut_kernel, in_specs=[IN_VMEM] * 4 + [IN_SMEM], out_specs=...  7.5 us
    ppermute x2, starting transfers between devices, section(): got_sums[g].append(lax.ppermute(part, 'inst', hop))  4.65 us
    ppermute x1, waiting for transfers between devices, section(): lax.ppermute(held, 'inst', swap)  4.54 us
    pallas_call x3, Pallas kernels, finish(): pl.pallas_call(functools.partial(finish_kernel, [(w, p, len(got)) for w,...  4.5 us
    pallas_call x1, Pallas kernels, stencil(): pl.pallas_call(functools.partial(stencil_kernel, period), in_specs=[IN_VM...  4.4 us
    ppermute x2, starting transfers between devices, section(): got_state = [[lax.ppermute(p, 'inst', hop) for hop in hops] for p in packed]  2.16 us
    pallas_call x1, Pallas kernels, pack_edges(): pl.pallas_call(pack_edges_kernel, in_specs=[IN_HBM], out_specs=[IN_VMEM]...  1.85 us
  transfers between devices with their start and end apart: 9, of which 3 were waited for; matrix products, arithmetic and copies ran while one was open for 0% of the time, Pallas kernels for 30%

profile of v5, /device:TPU:0, one launch (start us, length us, event | category | flops | bytes accessed | tf_op | source)
XLA Modules:
  0.0 56.4 jit_solution(9725127739144346784)
XLA Ops:
  0.6 1.9 %pack_edges.1 = (f32[4,5,8,4096]{3,2,1,0:T(8,128)S(1)}, bf16[5,8,4096]{2,1,0:T(8,128)(2,1)S(1)}, bf16[5,8,4096]{2,1,0:T(8,128)(2,1)S(1)}) custom-call(f32[4,5,8,4096]{3,2,1,0:T(8,128)} %state_ref.3), custom_call_target="tpu_custom_call" | custom-call | tf_op jit(solution)/shard_map/pack_edges/pallas_call | solution.py:159
  2.5 0.6 collective-permute-start
  3.0 4.5 %collective-permute-done.mate_ref = f32[4,5,8,4096]{3,2,1,0:T(8,128)S(1)} collective-permute-done((f32[4,5,8,4096]{3,2,1,0:T(8,128)S(1)}, f32[4,5,8,4096]{3,2,1,0:T(8,128)S(1)}, u32[]{:S(2)}, u32[]{:S(2)}) %collective-permute-start) | collective-permute-done | bytes 2621472 | tf_op jit(solution)/shard_map/ppermute | solution.py:459
  7.6 1.3 %send_sums.1 = (bf16[32,10240]{1,0:T(8,128)(2,1)S(1)}, bf16[32,2048]{1,0:T(8,128)(2,1)S(1)}) custom-call(f32[4,5,8,4096]{3,2,1,0:T(8,128)S(1)} %get-tuple-element.11.state_ref, f32[4,5,8,4096]{3,2,1,0:T(8,128)S(1)} %collective-permute-done.mate_ref), custom_call_target="tpu_custom_call" | custom-call | tf_op jit(solution)/shard_map/send_sums/pallas_call | solution.py:200
  8.9 0.0 copy-start
  8.9 0.0 copy-start.2
  8.9 0.0 copy-start.3
  8.9 0.0 copy-start.4
  9.0 2.9 %collective-permute-start.4 = (bf16[32,10240]{1,0:T(8,128)(2,1)S(1)}, bf16[32,10240]{1,0:T(8,128)(2,1)S(1)}, u32[]{:S(2)}, u32[]{:S(2)}) collective-permute-start(bf16[32,10240]{1,0:T(8,128)(2,1)S(1)} %get-tuple-element.15), channel_id=1, source_target_pairs={{0,8},{4,12},{8,0},{12,4},{1,9},{5,13},{9,1},{13,5},{2,10},{6,14},... | collective-permute-start | bytes 1966088 | tf_op jit(solution)/shard_map/ppermute | solution.py:467
  11.9 1.2 %pack_state.1 = bf16[1,32,4096]{2,1,0:T(8,128)(2,1)S(1)} custom-call(f32[4,5,8,4096]{3,2,1,0:T(8,128)} %state_ref.3), custom_call_target="tpu_custom_call" | custom-call | tf_op jit(solution)/shard_map/pack_state/pallas_call | solution.py:100
  13.0 0.2 collective-permute-start.5
  13.2 0.2 pack_more.1
  13.4 2.0 %collective-permute-start.7 = (bf16[1,32,4096]{2,1,0:T(8,128)(2,1)S(1)}, bf16[1,32,4096]{2,1,0:T(8,128)(2,1)S(1)}, u32[]{:S(2)}, u32[]{:S(2)}) collective-permute-start(bf16[1,32,4096]{2,1,0:T(8,128)(2,1)S(1)} %pack_more.1), channel_id=1, source_target_pairs={{0,8},{4,12},{8,0},{12,4},{1,9},{5,13},{9,1},{13,5},{2,10},{6,14},... | collective-permute-start | bytes 786440 | tf_op jit(solution)/shard_map/ppermute | solution.py:458
  15.4 1.6 %collective-permute-start.1 = (bf16[5,8,4096]{2,1,0:T(8,128)(2,1)S(1)}, bf16[5,8,4096]{2,1,0:T(8,128)(2,1)S(1)}, u32[]{:S(2)}, u32[]{:S(2)}) collective-permute-start(bf16[5,8,4096]{2,1,0:T(8,128)(2,1)S(1)} %get-tuple-element.12), channel_id=1, source_target_pairs={{0,1},{2,3},{1,0},{3,2},{4,5},{6,7},{5,4},{7,6},{8,9},{10,11},{9,8... | collective-permute-start | bytes 983048 | tf_op jit(solution)/shard_map/ppermute | solution.py:462
  16.9 0.7 %collective-permute-start.2 = (bf16[5,8,4096]{2,1,0:T(8,128)(2,1)S(1)}, bf16[5,8,4096]{2,1,0:T(8,128)(2,1)S(1)}, u32[]{:S(2)}, u32[]{:S(2)}) collective-permute-start(bf16[5,8,4096]{2,1,0:T(8,128)(2,1)S(1)} %get-tuple-element.13), channel_id=1, source_target_pairs={{1,2},{2,1},{5,6},{6,5},{9,10},{10,9},{13,14},{14,13},{17,18},{18,... | collective-permute-start | bytes 983048 | tf_op jit(solution)/shard_map/ppermute | solution.py:463
  17.6 15.4 %collective-permute-done.5.refs_0_ = bf16[1,32,4096]{2,1,0:T(8,128)(2,1)S(1)} collective-permute-done((bf16[1,32,4096]{2,1,0:T(8,128)(2,1)S(1)}, bf16[1,32,4096]{2,1,0:T(8,128)(2,1)S(1)}, u32[]{:S(2)}, u32[]{:S(2)}) %collective-permute-start.5) | collective-permute-done | bytes 262176 | tf_op jit(solution)/shard_map/ppermute | solution.py:458
  33.1 0.0 collective-permute-start.6
  33.1 5.1 %collective-permute-done.7.refs_2_ = bf16[1,32,4096]{2,1,0:T(8,128)(2,1)S(1)} collective-permute-done((bf16[1,32,4096]{2,1,0:T(8,128)(2,1)S(1)}, bf16[1,32,4096]{2,1,0:T(8,128)(2,1)S(1)}, u32[]{:S(2)}, u32[]{:S(2)}) %collective-permute-start.7) | collective-permute-done | bytes 262176 | tf_op jit(solution)/shard_map/ppermute | solution.py:458
  38.1 0.0 collective-permute-start.8
  38.1 0.0 collective-permute-done.1.first_ref
  38.1 1.7 %collective-permute-start.3 = (bf16[32,2048]{1,0:T(8,128)(2,1)S(1)}, bf16[32,2048]{1,0:T(8,128)(2,1)S(1)}, u32[]{:S(2)}, u32[]{:S(2)}) collective-permute-start(bf16[32,2048]{1,0:T(8,128)(2,1)S(1)} %get-tuple-element.14), channel_id=1, source_target_pairs={{0,8},{4,12},{8,0},{12,4},{1,9},{5,13},{9,1},{13,5},{2,10},{6,14},... | collective-permute-start | bytes 393224 | tf_op jit(solution)/shard_map/ppermute | solution.py:467
  39.9 0.0 copy-done
  39.9 0.0 copy-done.2
  39.9 0.0 copy-done.3
  39.9 0.0 copy-done.4
  39.9 7.5 %cut_terms.1.cut_ref = f32[512,1536]{1,0:T(8,128)S(1)} custom-call(f32[4,5,8,4096]{3,2,1,0:T(8,128)S(1)} %get-tuple-element.11.state_ref, bf16[8,320,320]{2,1,0:T(8,128)(2,1)S(1)} %copy-done, s32[1,256]{1,0:T(1,128)S(1)} %copy-done.2, s32[1,256]{1,0:T(1,128)S(1)} %copy-done.3, s32[4]{0:T(128)S(1)} %copy-done.4), custom_call_target="tpu_custom_call" | custom-call | tf_op jit(solution)/shard_map/cut_terms/pallas_call | solution.py:290
  47.4 0.0 copy-start.1
  47.4 0.0 collective-permute-done.2.second_ref
  47.4 4.4 %stencil.1.part_ref = f32[4,5,8,4096]{3,2,1,0:T(8,128)S(1)} custom-call(f32[4,5,8,4096]{3,2,1,0:T(8,128)S(1)} %get-tuple-element.11.state_ref, f32[4,5,8,4096]{3,2,1,0:T(8,128)S(1)} %collective-permute-done.mate_ref, f32[512,1536]{1,0:T(8,128)S(1)} %cut_terms.1.cut_ref, bf16[5,8,4096]{2,1,0:T(8,128)(2,1)S(1)} %collective-permute-done.1.first_ref, ...), custom_call_target="tpu_custom_call" | custom-call | tf_op jit(solution)/shard_map/stencil/pallas_call | solution.py:361
  51.8 0.0 collective-permute-done.6.refs_1_
  51.8 0.0 collective-permute-done.8.refs_3_
  51.8 0.0 copy-done.1
  51.9 1.9 %finish.3 = (f32[4,5,8,4096]{3,2,1,0:T(8,128)}, f32[4,5,8,4096]{3,2,1,0:T(8,128)}) custom-call(f32[4,5,8,4096]{3,2,1,0:T(8,128)S(1)} %stencil.1.part_ref, f32[4,5,8,4096]{3,2,1,0:T(8,128)S(1)} %get-tuple-element.11.state_ref, f32[8,4096]{1,0:T(8,128)S(1)} %copy-done.1, bf16[1,32,4096]{2,1,0:T(8,128)(2,1)S(1)} %collective-permute-done.5.refs_0_, ...), custom_call_target="tpu_custom_call" | custom-call | tf_op jit(solution)/shard_map/finish/pallas_call | solution.py:430
  53.7 0.0 collective-permute-done.4.refs_0_
  53.8 1.7 %finish.4 = (f32[4,5,8,4096]{3,2,1,0:T(8,128)}, f32[4,5,8,4096]{3,2,1,0:T(8,128)}) custom-call(f32[4,5,8,4096]{3,2,1,0:T(8,128)S(1)} %stencil.1.part_ref, f32[4,5,8,4096]{3,2,1,0:T(8,128)S(1)} %get-tuple-element.11.state_ref, f32[8,4096]{1,0:T(8,128)S(1)} %copy-done.1, ...), custom_call_target="tpu_custom_call", output_to_operand_aliasing={{0}: (4, {}), {1}: (5, {})} | custom-call | tf_op jit(solution)/shard_map/finish/pallas_call | solution.py:430
  55.5 0.0 collective-permute-done.3.refs_0_
  55.5 0.9 %finish.5 = (f32[4,5,8,4096]{3,2,1,0:T(8,128)}, f32[4,5,8,4096]{3,2,1,0:T(8,128)}) custom-call(f32[4,5,8,4096]{3,2,1,0:T(8,128)S(1)} %stencil.1.part_ref, f32[4,5,8,4096]{3,2,1,0:T(8,128)S(1)} %get-tuple-element.11.state_ref, f32[8,4096]{1,0:T(8,128)S(1)} %copy-done.1, ...), custom_call_target="tpu_custom_call", output_to_operand_aliasing={{0}: (4, {}), {1}: (5, {})} | custom-call | tf_op jit(solution)/shard_map/finish/pallas_call | solution.py:430
Async XLA Ops:
  2.5 5.1 %collective-permute-start = (f32[4,5,8,4096]{3,2,1,0:T(8,128)S(1)}, f32[4,5,8,4096]{3,2,1,0:T(8,128)S(1)}, u32[]{:S(2)}, u32[]{:S(2)}) collective-permute-start(f32[4,5,8,4096]{3,2,1,0:T(8,128)S(1)} %get-tuple-element.11.state_ref), channel_id=1, source_target_pairs={{0,4},{4,0},{8,12},{12,8},{1,5},{5,1},{9,13},{13,9},{2,6},{6,2},{1... | collective-permute-start | bytes 7864328 | tf_op jit(solution)/shard_map/ppermute | solution.py:459
  8.9 31.0 %copy-start = (bf16[8,320,320]{2,1,0:T(8,128)(2,1)S(1)}, bf16[8,320,320]{2,1,0:T(8,128)(2,1)}, u32[]{:S(2)}) copy-start(bf16[8,320,320]{2,1,0:T(8,128)(2,1)} %blocks_ref.1) | copy-start | bytes 4915204
  8.9 31.0 %copy-start.2 = (s32[1,256]{1,0:T(1,128)S(1)}, s32[1,256]{1,0:T(1,128)}, u32[]{:S(2)}) copy-start(s32[1,256]{1,0:T(1,128)} %index_ref.1) | copy-start | bytes 3076
  8.9 31.0 %copy-start.3 = (s32[1,256]{1,0:T(1,128)S(1)}, s32[1,256]{1,0:T(1,128)}, u32[]{:S(2)}) copy-start(s32[1,256]{1,0:T(1,128)} %type_ref.1) | copy-start | bytes 3076
  8.9 31.0 %copy-start.4 = (s32[4]{0:T(128)S(1)}, s32[4]{0:T(128)}, u32[]{:S(2)}) copy-start(s32[4]{0:T(128)} %count_ref.1) | copy-start | bytes 52
  9.0 44.8 %collective-permute-start.4 = (bf16[32,10240]{1,0:T(8,128)(2,1)S(1)}, bf16[32,10240]{1,0:T(8,128)(2,1)S(1)}, u32[]{:S(2)}, u32[]{:S(2)}) collective-permute-start(bf16[32,10240]{1,0:T(8,128)(2,1)S(1)} %get-tuple-element.15), channel_id=1, source_target_pairs={{0,8},{4,12},{8,0},{12,4},{1,9},{5,13},{9,1},{13,5},{2,10},{6,14},... | collective-permute-start | bytes 1966088 | tf_op jit(solution)/shard_map/ppermute | solution.py:467
  13.0 20.0 %collective-permute-start.5 = (bf16[1,32,4096]{2,1,0:T(8,128)(2,1)S(1)}, bf16[1,32,4096]{2,1,0:T(8,128)(2,1)S(1)}, u32[]{:S(2)}, u32[]{:S(2)}) collective-permute-start(bf16[1,32,4096]{2,1,0:T(8,128)(2,1)S(1)} %pack_state.1), channel_id=1, source_target_pairs={{0,8},{4,12},{8,0},{12,4},{1,9},{5,13},{9,1},{13,5},{2,10},{6,14},... | collective-permute-start | bytes 786440 | tf_op jit(solution)/shard_map/ppermute | solution.py:458
  13.4 24.7 %collective-permute-start.7 = (bf16[1,32,4096]{2,1,0:T(8,128)(2,1)S(1)}, bf16[1,32,4096]{2,1,0:T(8,128)(2,1)S(1)}, u32[]{:S(2)}, u32[]{:S(2)}) collective-permute-start(bf16[1,32,4096]{2,1,0:T(8,128)(2,1)S(1)} %pack_more.1), channel_id=1, source_target_pairs={{0,8},{4,12},{8,0},{12,4},{1,9},{5,13},{9,1},{13,5},{2,10},{6,14},... | collective-permute-start | bytes 786440 | tf_op jit(solution)/shard_map/ppermute | solution.py:458
  15.4 22.8 %collective-permute-start.1 = (bf16[5,8,4096]{2,1,0:T(8,128)(2,1)S(1)}, bf16[5,8,4096]{2,1,0:T(8,128)(2,1)S(1)}, u32[]{:S(2)}, u32[]{:S(2)}) collective-permute-start(bf16[5,8,4096]{2,1,0:T(8,128)(2,1)S(1)} %get-tuple-element.12), channel_id=1, source_target_pairs={{0,1},{2,3},{1,0},{3,2},{4,5},{6,7},{5,4},{7,6},{8,9},{10,11},{9,8... | collective-permute-start | bytes 983048 | tf_op jit(solution)/shard_map/ppermute | solution.py:462
  16.9 30.5 %collective-permute-start.2 = (bf16[5,8,4096]{2,1,0:T(8,128)(2,1)S(1)}, bf16[5,8,4096]{2,1,0:T(8,128)(2,1)S(1)}, u32[]{:S(2)}, u32[]{:S(2)}) collective-permute-start(bf16[5,8,4096]{2,1,0:T(8,128)(2,1)S(1)} %get-tuple-element.13), channel_id=1, source_target_pairs={{1,2},{2,1},{5,6},{6,5},{9,10},{10,9},{13,14},{14,13},{17,18},{18,... | collective-permute-start | bytes 983048 | tf_op jit(solution)/shard_map/ppermute | solution.py:463
  33.1 18.8 %collective-permute-start.6 = (bf16[1,32,4096]{2,1,0:T(8,128)(2,1)S(1)}, bf16[1,32,4096]{2,1,0:T(8,128)(2,1)S(1)}, u32[]{:S(2)}, u32[]{:S(2)}) collective-permute-start(bf16[1,32,4096]{2,1,0:T(8,128)(2,1)S(1)} %collective-permute-done.5.refs_0_), channel_id=1, source_target_pairs={{0,4},{4,0},{8,12},{12,8},{1,5},{5,1},{9,13},{13,9},{2,6},{6,2},{1... | collective-permute-start | bytes 786440 | tf_op jit(solution)/shard_map/ppermute | solution.py:474
  38.1 13.7 %collective-permute-start.8 = (bf16[1,32,4096]{2,1,0:T(8,128)(2,1)S(1)}, bf16[1,32,4096]{2,1,0:T(8,128)(2,1)S(1)}, u32[]{:S(2)}, u32[]{:S(2)}) collective-permute-start(bf16[1,32,4096]{2,1,0:T(8,128)(2,1)S(1)} %collective-permute-done.7.refs_2_), channel_id=1, source_target_pairs={{0,4},{4,0},{8,12},{12,8},{1,5},{5,1},{9,13},{13,9},{2,6},{6,2},{1... | collective-permute-start | bytes 786440 | tf_op jit(solution)/shard_map/ppermute | solution.py:474
  38.1 17.3 %collective-permute-start.3 = (bf16[32,2048]{1,0:T(8,128)(2,1)S(1)}, bf16[32,2048]{1,0:T(8,128)(2,1)S(1)}, u32[]{:S(2)}, u32[]{:S(2)}) collective-permute-start(bf16[32,2048]{1,0:T(8,128)(2,1)S(1)} %get-tuple-element.14), channel_id=1, source_target_pairs={{0,8},{4,12},{8,0},{12,4},{1,9},{5,13},{9,1},{13,5},{2,10},{6,14},... | collective-permute-start | bytes 393224 | tf_op jit(solution)/shard_map/ppermute | solution.py:467
  47.4 4.4 %copy-start.1 = (f32[8,4096]{1,0:T(8,128)S(1)}, f32[8,4096]{1,0:T(8,128)}, u32[]{:S(2)}) copy-start(f32[8,4096]{1,0:T(8,128)} %step_ref.5) | copy-start | bytes 393220
